TPU v7x, 128 devices: a whole 4x4x4 slice. The times are simulated.
128 devices in a mesh: shard: 32 (over y, z_hi, x), tensor: 4 (over z_lo, core).
Axes of the slice: x: 4, y: 4, z: 4 (z_hi: 2, z_lo: 2; z = z_hi * 2 + z_lo), core: 2. Of those that a mesh axis runs over, the one named last changes fastest.
Arguments:
- acts: bfloat16 [32768, 768], P('shard', 'tensor')
- out_grads: bfloat16 [2, 32768, 768], P(None, 'shard', 'tensor')
- sampled_rows: int32 [2, 262144], P(None, 'shard'), may hold values from 0 to 1023
- proj_grad: float32 [768, 768], P(('shard', 'tensor')), may hold values from -600 to 600
- proj_momentum: float32 [768, 768], P(('shard', 'tensor')), may hold values from -6 to 6
- embed_grad: float32 [49152, 768], P(('shard', 'tensor')), may hold values from -36 to 36
- embed_momentum: float32 [49152, 768], P(('shard', 'tensor')), may hold values from -6 to 6
- token_counts: int32 [49152], P(('shard', 'tensor')), may hold values from 0 to 99
Outputs:
- proj_momentum_new: float32 [768, 768], P(('shard', 'tensor'))
- embed_momentum_new: float32 [49152, 768], P(('shard', 'tensor'))
Inputs may be any that keep to these rules, and one draw needn't show every extreme that they name: `sampled_rows`: entry j of a row picks token (j // 8192) * 1024 + value, one of the 1024 tokens of its index of shard; repeats are allowed.
All inputs are finite; a program needn't handle non-finite values.
Results may differ from a plain program's by a relative error of at most 0.0003.
Values may be sent and summed in bfloat16 or wider, within the bound.
No kernel may reach another device: no remote copies, remote signals or barrier semaphores. Data moves between devices by JAX's collectives and lax.ppermute only.
A program may use at most 128 MiB of HBM per device.

v0:
```python
import jax
import jax.numpy as jnp
from jax import lax
from jax.sharding import PartitionSpec as P

D = 768
VOCAB = 49152
SAMPLE = 2048
NS_ITERS = 3


momentum_decay = 0.9
damping_root = 0.5
count_scale = 64.0
highest = lax.Precision.HIGHEST


def per_device(
    acts,
    out_grads,
    sampled_rows,
    proj_grad,
    proj_momentum,
    embed_grad,
    embed_momentum,
    token_counts,
):
    n_shard = lax.axis_size("shard")
    n_tensor = lax.axis_size("tensor")
    devices_all = n_shard * n_tensor
    flat_index = lax.axis_index("shard") * n_tensor + lax.axis_index("tensor")
    width = D
    row_count = width // devices_all
    sample_total = SAMPLE * devices_all
    picked = jnp.stack(
        [
            jnp.take(acts, sampled_rows[0], axis=0),
            jnp.take(out_grads[0], sampled_rows[0], axis=0),
            jnp.take(out_grads[1], sampled_rows[1], axis=0),
        ]
    )
    sampled = lax.all_to_all(picked, "tensor", split_axis=1, concat_axis=2, tiled=True)
    trace_part = jnp.sum(jnp.square(sampled.astype(jnp.float32)), axis=(1, 2))
    factor_rows = (
        lax.psum_scatter(
            jnp.einsum("fsd,fse->dfe", sampled, sampled, preferred_element_type=jnp.float32),
            ("shard", "tensor"),
            scatter_dimension=0,
            tiled=True,
        )
        / sample_total
    )
    frob_part = jnp.sum(factor_rows * factor_rows, axis=(0, 2))
    count_part = jnp.sum(token_counts).astype(jnp.float32)
    frob_total, trace_total, count_total = lax.psum(
        (frob_part, trace_part, count_part), ("shard", "tensor")
    )
    traces = trace_total / sample_total
    ratio = jnp.sqrt(traces[0] / traces[1])
    embed_ratio = jnp.sqrt(count_total / count_scale / VOCAB / (traces[2] / width))
    shifts = jnp.stack([damping_root * ratio, damping_root / ratio, damping_root / embed_ratio])
    norm_sq = frob_total + 2.0 * shifts * traces + width * shifts * shifts
    start_scale = 1.0 / jnp.sqrt(norm_sq)
    row_ids = flat_index * row_count + jnp.arange(row_count, dtype=jnp.int32)
    eye_rows = (jnp.arange(width, dtype=jnp.int32)[None, :] == row_ids[:, None]).astype(
        jnp.float32
    )[:, None, :]
    damped = factor_rows + shifts[None, :, None] * eye_rows
    rows_now = (
        2.0 * start_scale[None, :, None] * eye_rows
        - (start_scale * start_scale)[None, :, None] * damped
    )
    for iteration in range(NS_ITERS):
        inverses = lax.all_gather(rows_now, ("shard", "tensor"), axis=0, tiled=True)
        if iteration < NS_ITERS - 1:
            product = jnp.einsum("rfk,kfj->rfj", damped, inverses, precision=highest)
            rows_now = 2.0 * rows_now - jnp.einsum(
                "rfk,kfj->rfj", product, inverses, precision=highest
            )
    g_inverse = inverses[:, 1, :]
    e_inverse = inverses[:, 2, :]
    a_rows = lax.dynamic_slice_in_dim(inverses[:, 0, :], flat_index * row_count, row_count, 0)
    mixed_rows = jnp.dot(proj_grad, g_inverse, precision=highest)
    update = jnp.dot(
        a_rows,
        lax.all_gather(mixed_rows, ("shard", "tensor"), axis=0, tiled=True),
        precision=highest,
    )
    row_scale = token_counts.astype(jnp.float32) / count_scale + damping_root * embed_ratio
    embed_update = jnp.dot(embed_grad, e_inverse, precision=highest) / row_scale[:, None]
    return (momentum_decay * proj_momentum + update, momentum_decay * embed_momentum + embed_update)


def solution(mesh):
    return jax.shard_map(
        per_device,
        mesh=mesh,
        in_specs=(
            P("shard", "tensor"),
            P(None, "shard", "tensor"),
            P(None, "shard"),
            P(("shard", "tensor"), None),
            P(("shard", "tensor"), None),
            P(("shard", "tensor"), None),
            P(("shard", "tensor"), None),
            P(("shard", "tensor")),
        ),
        out_specs=(P(("shard", "tensor"), None), P(("shard", "tensor"), None)),
        check_vma=False,
    )
```

profile of v0, /device:TPU:1, one launch (start us, length us, event | category | flops | bytes accessed | tf_op | source)
XLA Modules:
  0.0 1490.3 jit_solution(11976387362760375360)
XLA Ops:
  7.2 1.0 fusion.62
  8.3 1.2 copy.48
  9.5 1.2 fusion.61
  10.7 0.2 copy.72
  10.9 0.2 copy.73
  11.1 32.9 %gather_fusion.1 = bf16[8192,192]{1,0:T(8,128)(2,1)} fusion(bf16[1024,192]{1,0:T(8,128)(2,1)S(1)} %bitcast.65, s32[8192]{0:T(1024)S(1)} %fusion.50), kind=kCustom, calls=%fused_computation.1.clone | custom fusion | bytes 6324224 | tf_op jit(solution)/shard_map/jit(_take)/gather | solution.py:38
  44.0 32.9 %gather_fusion = bf16[8192,192]{1,0:T(8,128)(2,1)} fusion(bf16[1024,192]{1,0:T(8,128)(2,1)S(1)} %copy.48, s32[8192]{0:T(1024)S(1)} %fusion.50), kind=kCustom, calls=%fused_computation.clone | custom fusion | bytes 6324224 | tf_op jit(solution)/shard_map/jit(_take)/gather | solution.py:37
  76.9 32.9 %gather_fusion.2 = bf16[8192,192]{1,0:T(8,128)(2,1)} fusion(bf16[1024,192]{1,0:T(8,128)(2,1)S(1)} %bitcast.64, s32[8192]{0:T(1024)S(1)} %fusion.51), kind=kCustom, calls=%fused_computation.2.clone | custom fusion | bytes 6324224 | tf_op jit(solution)/shard_map/jit(_take)/gather | solution.py:39
  109.9 6.8 select_bitcast_fusion
  116.7 4.3 select_bitcast_fusion.2
  121.0 6.2 pad_maximum_fusion
  127.2 17.9 %copy.51 = bf16[3,8192,192]{2,0,1:T(4,128)(2,1)S(1)} copy(bf16[3,8192,192]{2,1,0:T(8,128)(2,1)} %pad_maximum_fusion) | data formatting | bytes 18874368 | tf_op jit(solution)/shard_map/stack | solution.py:35
  145.1 187.8 %all_to_all.18 = bf16[3,8192,192]{2,0,1:T(4,128)(2,1)} all-to-all(bf16[3,8192,192]{2,0,1:T(4,128)(2,1)S(1)} %copy.51), channel_id=1, replica_groups=mesh['shard'=32,'tensor'=4] {'tensor'}, dimensions={1} | all-to-all | bytes 18874368 | tf_op jit(solution)/shard_map/all_to_all | solution.py:42
  332.8 24.3 %copy.53 = bf16[3,2048,4,192]{1,3,2,0:T(8,128)(2,1)} copy(bf16[3,2048,4,192]{3,0,1,2:T(4,128)(2,1)} %bitcast.66) | data formatting | bytes 18874368 | tf_op jit(solution)/shard_map/all_to_all | solution.py:42
  357.1 14.6 convolution_bitcast_fusion
  371.8 11.0 copy.55
  382.8 0.3 all-gather.6.cloned.1.call-start
  383.0 0.4 copy-done.3
  383.4 0.6 reduce_sum.29
  384.7 26.5 %copy.67 = bf16[3,4,2048,192]{2,1,3,0:T(4,128)(2,1)} copy(bf16[3,4,2048,192]{3,0,2,1:T(4,128)(2,1)} %bitcast.67) | data formatting | bytes 18874368 | tf_op jit(solution)/shard_map/all_to_all | solution.py:42
  411.3 10.6 multiply_reduce_fusion
  421.9 127.7 %all-reduce.4.cloned.1.call-done = f32[768,3,768]{2,1,0:T(4,128)} async-done(((f32[768,3,768]{2,1,0:T(4,128)}), f32[768,3,768]{2,1,0:T(4,128)}) %all-reduce.4.cloned.1.call-update) | async-done | bytes 7077904
  549.6 0.9 constant_dynamic-slice_fusion
  550.5 0.1 multiply_reduce_fusion.1
  550.6 64.2 %all-reduce.1 = (f32[]{:T(128)}, f32[3]{0:T(128)S(1)}, f32[3]{0:T(128)S(1)}) all-reduce(f32[]{:T(128)S(6)} %convert_element_type.18, f32[3]{0:T(128)S(1)} %multiply_reduce_fusion, f32[3]{0:T(128)S(1)} %multiply_reduce_fusion.1), channel_id=1, replica_groups=mesh['shard'=32,'tensor'=4] {'shard','tensor'}, use_global_device_ids=true, to_apply=%region_6.8 | all-reduce | flops 7 | bytes 56 | tf_op jit(solution)/shard_map/psum | solution.py:55
  614.8 0.6 fusion.63
  618.5 0.7 copy.57
  619.2 0.3 all-gather.8.cloned.1.call-start
  619.5 201.8 %all-gather.6.cloned.1.call-done = f32[768,3,768]{2,1,0:T(4,128)} async-done(((f32[6,3,768]{2,1,0:T(4,128)}), f32[768,3,768]{2,1,0:T(4,128)}) %all-gather.6.cloned.1.call-update) | async-done | bytes 7077904 | tf_op jit(solution)/shard_map/all_gather | solution.py:74
  821.3 7.9 fusion.29
  829.3 7.9 fusion.26
  837.2 0.7 copy.60
  837.9 0.5 all-gather.10.cloned.1.call-start
  838.4 203.9 %all-gather.8.cloned.1.call-done = f32[768,3,768]{2,1,0:T(4,128)} async-done(((f32[6,3,768]{2,1,0:T(4,128)}), f32[768,3,768]{2,1,0:T(4,128)}) %all-gather.8.cloned.1.call-update) | async-done | bytes 7077904 | tf_op jit(solution)/shard_map/all_gather | solution.py:74
  1042.3 7.9 fusion.38
  1050.2 7.9 fusion.35
  1058.1 0.7 copy.63
  1058.8 0.2 all-gather.12.cloned.1.call-start
  1059.0 204.1 %all-gather.10.cloned.1.call-done = f32[768,3,768]{2,1,0:T(4,128)} async-done(((f32[6,3,768]{2,1,0:T(4,128)}), f32[768,3,768]{2,1,0:T(4,128)}) %all-gather.10.cloned.1.call-update) | async-done | bytes 7077904 | tf_op jit(solution)/shard_map/all_gather | solution.py:74
  1263.2 16.8 %fusion.60 = (f32[768,1,768]{2,1,0:T(1,128)}, f32[768,1,768]{2,1,0:T(1,128)S(1)}, f32[768,1,768]{2,1,0:T(1,128)S(1)}) fusion(f32[768,3,768]{2,1,0:T(4,128)} %all-gather.10.cloned.1.call-done), kind=kLoop, calls=%fused_computation.66 | loop fusion | bytes 14155776 | tf_op jit(solution)/shard_map/slice | solution.py:81
  1280.0 2.7 fusion.41
  1282.7 2.7 copy.64
  1285.3 10.5 fusion.20
  1295.8 2.7 copy.65
  1298.5 0.6 constant_dynamic-slice_fusion.1
  1299.1 179.3 %all-gather.12.cloned.1.call-done = f32[128,6,768]{2,1,0:T(8,128)} async-done(((f32[1,6,768]{2,1,0:T(8,128)}), f32[128,6,768]{2,1,0:T(8,128)}) %all-gather.12.cloned.1.call-update) | async-done | bytes 2359312 | tf_op jit(solution)/shard_map/all_gather | solution.py:86
  1478.4 2.7 reshape.75
  1481.0 2.6 convolution_add_fusion
  (24 shorter events, 0.5 us)
Async XLA Ops:
  7.2 1278.2 %copy-start = (f32[384,768]{1,0:T(8,128)S(1)}, f32[384,768]{1,0:T(8,128)}, u32[]{:S(2)}) copy-start(f32[384,768]{1,0:T(8,128)} %param.15) | copy-start | bytes 3538948
  7.2 542.4 %all-reduce.4.cloned.1.call-start = ((), (), s32[]{:S(2)}) async-start(), calls=%async_computation.5 | async-start | bytes 18874368
  109.9 6.8 copy-start.1
  109.9 6.9 copy-start.2
  382.7 0.7 copy-start.3
  382.8 438.5 %all-gather.6.cloned.1.call-start = ((), (), s32[]{:S(2)}) async-start(), calls=%async_computation.1 | async-start | bytes 9510912 | tf_op jit(solution)/shard_map/all_gather | solution.py:74
  619.2 423.1 %all-gather.8.cloned.1.call-start = ((), (), s32[]{:S(2)}) async-start(), calls=%async_computation.2 | async-start | bytes 9510912 | tf_op jit(solution)/shard_map/all_gather | solution.py:74
  837.9 425.3 %all-gather.10.cloned.1.call-start = ((), (), s32[]{:S(2)}) async-start(), calls=%async_computation.3 | async-start | bytes 9510912 | tf_op jit(solution)/shard_map/all_gather | solution.py:74
  1058.8 419.6 %all-gather.12.cloned.1.call-start = ((), (), s32[]{:S(2)}) async-start(), calls=%async_computation.4 | async-start | bytes 3170304 | tf_op jit(solution)/shard_map/all_gather | solution.py:86
Sparse Core Ops, SparseCore 0:
  382.9 166.6 all-reduce.3
  619.3 201.9 all-gather.5
  838.0 204.2 all-gather.7
  1058.9 204.1 all-gather.9
  1282.8 195.5 all-gather.11
where the time goes:
time: 1500 us; the launch traced here: 1490 us
  waiting for transfers between devices  917 us (61%)
  blocking collectives  252 us (17%)
  local copies, waits for them, and re-layouts  212 us (14%)
  matrix products  62.1 us (4%)
  other arithmetic  29 us (2%)
  between operations  17.6 us (1%)
    all_gather x3, waiting for transfers between devices, per_device(): inverses = lax.all_gather(rows_now, ('shard', 'tensor'), axis=0, tiled=True)  610 us
    all_to_all x1, blocking collectives, per_device(): lax.all_to_all(picked, 'tensor', split_axis=1, concat_axis=2, tiled=True)  188 us
    all_gather x1, waiting for transfers between devices, per_device(): lax.all_gather(mixed_rows, ('shard', 'tensor'), axis=0, tiled=True)  179 us
    unnamed x6, waiting for transfers between devices  128 us
    psum x1, blocking collectives, per_device(): lax.psum((frob_part, trace_part, count_part), ('shard', 'tensor'))  64.2 us
    all_to_all x2, local copies, waits for them, and re-layouts, per_device(): lax.all_to_all(picked, 'tensor', split_axis=1, concat_axis=2, tiled=True)  50.8 us
    gather x1, local copies, waits for them, and re-layouts, per_device(): jnp.take(out_grads[0], sampled_rows[0], axis=0)  32.9 us
    gather x1, local copies, waits for them, and re-layouts, per_device(): jnp.take(out_grads[1], sampled_rows[1], axis=0)  32.9 us
  transfers between devices with their start and end apart: 5, of which 5 were waited for; matrix products, arithmetic and copies ran while one was open for 4% of the time, Pallas kernels for 0%

commit v1 on v0

v1 whole, which is shorter than its diff:
```python
import jax
import jax.numpy as jnp
from jax import lax
from jax.experimental import pallas as pl
from jax.experimental.pallas import tpu as pltpu
from jax.sharding import Mesh, PartitionSpec as P

D = 768
VOCAB = 49152
TOK = 1024
SAMPLES = 262144
BLK = 128
NB = D // BLK
CHIPS = 64
HALF = BLK // 2
STEPS = 7

momentum_decay = 0.9
damping_root = 0.5
count_scale = 64.0

CHIP_AXES = ("y", "zh", "x", "zl")
f32 = jnp.float32
bf16 = jnp.bfloat16

BLOCKS = [(f, i, j) for f in range(3) for i in range(NB) for j in range(i, NB)]


def vmem():
    return pl.BlockSpec(memory_space=pltpu.VMEM)


def smem():
    return pl.BlockSpec(memory_space=pltpu.SMEM)


def params():
    return pltpu.CompilerParams(vmem_limit_bytes=60 * 1024 * 1024)


def nt_dot(a, b):
    return lax.dot_general(a, b, (((1,), (1,)), ((), ())), preferred_element_type=f32)


def nn_dot(a, b):
    return lax.dot_general(a, b, (((1,), (0,)), ((), ())), preferred_element_type=f32)


def split(x):
    hi = x.astype(bf16)
    return hi, (x - hi.astype(f32)).astype(bf16)


def histogram_kernel(info, ids_ref, out_ref):
    first = info[0] * 4
    width = 1024
    high_rows = lax.broadcasted_iota(jnp.int32, (16, width), 0) + first
    low_rows = lax.broadcasted_iota(jnp.int32, (BLK, width), 0)
    for k in range(2):
        total = jnp.zeros((16, BLK), f32)
        for part in range(8):
            ids = ids_ref[k : k + 1, part * width : (part + 1) * width]
            high = (high_rows == (ids >> 7)).astype(f32).astype(bf16)
            low = (low_rows == (ids & 127)).astype(f32).astype(bf16)
            total = total + nt_dot(high, low)
        out_ref[k] = total


def gram_kernel(info, hist_ref, own_ref, own_c_ref, other_ref, other_c_ref, count_ref, out_ref, x_ref):
    zl, core = info[0], info[1]
    places = [2 * zl + core, 2 * zl + 1 - core, 2 * (1 - zl) + core, 2 * (1 - zl) + 1 - core]
    tokens = jnp.sum(count_ref[...].astype(f32), keepdims=True).reshape(1, 1)
    out_ref[CHIPS - 1] = jnp.broadcast_to(tokens, (HALF, BLK)).astype(out_ref.dtype)
    for f in range(3):
        for place, ref in zip(places, (own_ref, own_c_ref, other_ref, other_c_ref)):
            x_ref[pl.ds(pl.multiple_of(place * 192, 192), 192), :] = ref[f]
        x = x_ref[...]
        left = jnp.concatenate(
            [x_ref[pl.ds(pl.multiple_of(i * BLK + core * HALF, HALF), HALF), :] for i in range(NB)], axis=0
        )
        row = 1 if f == 2 else 0
        weight = jnp.concatenate([hist_ref[row, h : h + 1, :] for h in range(4)], axis=1)
        hi, lo = split(left.astype(f32) * weight)
        gram = nt_dot(hi, x) + nt_dot(lo, x)
        for b, (g, i, j) in enumerate(BLOCKS):
            if g == f:
                out_ref[b] = gram[i * HALF : (i + 1) * HALF, j * BLK : (j + 1) * BLK].astype(out_ref.dtype)


def total_kernel(in_ref, out_ref):
    total = jnp.sum(in_ref[...].astype(f32), axis=0) * (1.0 / SAMPLES)
    for s in range(CHIPS):
        out_ref[s] = total.astype(out_ref.dtype)


def step(y, start, hi_ref, lo_ref):
    y_hi, y_lo = split(y)
    hi, lo = hi_ref[...], lo_ref[...]
    return start + y - (nn_dot(y_hi, hi) + nn_dot(y_lo, hi) + nn_dot(y_hi, lo))


def finish_kernel(
    info, own_ref, other_ref, p_ref, p_mom_ref, g_ref, e_mom_ref, count_ref,
    p_out_ref, e_out_ref, full_ref, hi_ref, lo_ref, y_ref,
):
    core, flat = info[0], info[1]
    rows = lax.broadcasted_iota(jnp.int32, (BLK, BLK), 0)
    cols = lax.broadcasted_iota(jnp.int32, (BLK, BLK), 1)
    diagonal = rows == cols
    zero = jnp.zeros((BLK, BLK), f32)
    squares = [zero, zero, zero]
    traces = [zero, zero, zero]
    for b, (f, i, j) in enumerate(BLOCKS):
        for part, ref in ((core, own_ref), (1 - core, other_ref)):
            start = pl.multiple_of(i * BLK + part * HALF, HALF)
            full_ref[f, pl.ds(start, HALF), j * BLK : (j + 1) * BLK] = ref[b].astype(f32)
        block = full_ref[f, i * BLK : (i + 1) * BLK, j * BLK : (j + 1) * BLK]
        if i == j:
            squares[f] = squares[f] + block * block
            traces[f] = traces[f] + jnp.where(diagonal, block, 0.0)
        else:
            squares[f] = squares[f] + 2.0 * block * block
    squares = [jnp.sum(s, keepdims=True) for s in squares]
    traces = [jnp.sum(t, keepdims=True) for t in traces]
    tokens = (own_ref[CHIPS - 1][0:1, 0:1] + other_ref[CHIPS - 1][0:1, 0:1]) * float(SAMPLES)
    ratio = jnp.sqrt(traces[0] / traces[1])
    embed_ratio = jnp.sqrt(tokens / count_scale / VOCAB / (traces[2] / D))
    shifts = [damping_root * ratio, damping_root / ratio, damping_root / embed_ratio]
    scales = []
    for f in range(3):
        q = squares[f] + 2.0 * shifts[f] * traces[f] + D * shifts[f] * shifts[f]
        scales.append(1.0 / jnp.sqrt(q))
    for b, (f, i, j) in enumerate(BLOCKS):
        block = full_ref[f, i * BLK : (i + 1) * BLK, j * BLK : (j + 1) * BLK]
        if i == j:
            block = block + jnp.where(diagonal, shifts[f], 0.0)
        block = block * scales[f]
        hi, lo = split(block)
        hi_ref[f, i * BLK : (i + 1) * BLK, j * BLK : (j + 1) * BLK] = hi
        lo_ref[f, i * BLK : (i + 1) * BLK, j * BLK : (j + 1) * BLK] = lo
        if i != j:
            hi, lo = split(block.T)
            hi_ref[f, j * BLK : (j + 1) * BLK, i * BLK : (i + 1) * BLK] = hi
            lo_ref[f, j * BLK : (j + 1) * BLK, i * BLK : (i + 1) * BLK] = lo

    half = 192
    row = lax.broadcasted_iota(jnp.int32, (8, D), 0)
    col = lax.broadcasted_iota(jnp.int32, (8, D), 1)
    unit = jnp.where((row < 6) & (col == flat * 6 + row), 1.0, 0.0)

    def first(_, carry):
        a, y = carry
        a = step(a, unit, hi_ref.at[0], lo_ref.at[0])
        y = step(y, g_ref[0:half, :], hi_ref.at[2], lo_ref.at[2])
        return a, y

    a, y = lax.fori_loop(0, STEPS, first, (unit, g_ref[0:half, :]))
    y_ref[0:half, :] = y
    a_hi, a_lo = split(a * scales[0])
    p_hi, p_lo = split(p_ref[...])
    mixed = nn_dot(a_hi, p_hi) + nn_dot(a_lo, p_hi) + nn_dot(a_hi, p_lo)

    def second(_, carry):
        a, y = carry
        a = step(a, mixed, hi_ref.at[1], lo_ref.at[1])
        y = step(y, g_ref[half:, :], hi_ref.at[2], lo_ref.at[2])
        return a, y

    a, y = lax.fori_loop(0, STEPS, second, (mixed, g_ref[half:, :]))
    y_ref[half:, :] = y
    p_out_ref[...] = momentum_decay * p_mom_ref[...] + (a * scales[1])[0:6]
    row_scale = count_ref[...].astype(f32) / count_scale + damping_root * embed_ratio
    e_out_ref[...] = momentum_decay * e_mom_ref[...] + y_ref[...] * scales[2] / row_scale


def to_other(x, axis):
    return lax.ppermute(x, axis, [(0, 1), (1, 0)])


def exchange(x):
    return lax.all_to_all(x, CHIP_AXES, split_axis=0, concat_axis=0, tiled=True)


def per_device(acts, out_grads, sampled_rows, proj_grad, proj_momentum, embed_grad, embed_momentum, token_counts):
    zl, core = lax.axis_index("zl"), lax.axis_index("c")
    chip = lax.axis_index(CHIP_AXES)
    flat = chip * 2 + core

    features = jnp.concatenate([acts.T[None], jnp.transpose(out_grads, (0, 2, 1))], axis=0)
    keep = lax.dynamic_slice_in_dim(features, zl * 512, 512, 2)
    send = lax.dynamic_slice_in_dim(features, (1 - zl) * 512, 512, 2)
    other = to_other(send, "zl")
    keep_c = to_other(keep, "c")
    other_c = to_other(other, "c")

    hist = pl.pallas_call(
        histogram_kernel,
        out_shape=jax.ShapeDtypeStruct((2, 16, BLK), f32),
        in_specs=[smem(), vmem()],
        out_specs=vmem(),
        compiler_params=params(),
        name="histogram",
    )(jnp.stack([zl]), sampled_rows)

    parts = pl.pallas_call(
        gram_kernel,
        out_shape=jax.ShapeDtypeStruct((CHIPS, HALF, BLK), f32),
        in_specs=[smem()] + [vmem()] * 6,
        out_specs=vmem(),
        scratch_shapes=[pltpu.VMEM((D, 512), bf16)],
        compiler_params=params(),
        name="gram",
    )(jnp.stack([zl, core]), hist, keep, keep_c, other, other_c, token_counts.reshape(3, BLK))

    rows = proj_grad.shape[0]
    p_own = exchange(jnp.broadcast_to(proj_grad[None], (CHIPS,) + proj_grad.shape))
    p_other = to_other(p_own, "c")
    p_pair = jnp.stack([jnp.where(core == 0, p_own, p_other), jnp.where(core == 0, p_other, p_own)], axis=1)
    p_full = p_pair.reshape(D, D)

    arrived = exchange(parts)
    spread = pl.pallas_call(
        total_kernel,
        out_shape=jax.ShapeDtypeStruct((CHIPS, HALF, BLK), f32),
        in_specs=[vmem()],
        out_specs=vmem(),
        compiler_params=params(),
        name="total",
    )(arrived)
    own_blocks = exchange(spread)
    other_blocks = to_other(own_blocks, "c")

    return pl.pallas_call(
        finish_kernel,
        out_shape=(
            jax.ShapeDtypeStruct(proj_momentum.shape, f32),
            jax.ShapeDtypeStruct(embed_momentum.shape, f32),
        ),
        in_specs=[smem()] + [vmem()] * 7,
        out_specs=(vmem(), vmem()),
        scratch_shapes=[
            pltpu.VMEM((3, D, D), f32),
            pltpu.VMEM((3, D, D), bf16),
            pltpu.VMEM((3, D, D), bf16),
            pltpu.VMEM((384, D), f32),
        ],
        compiler_params=params(),
        name="finish",
    )(
        jnp.stack([core, flat]), own_blocks, other_blocks, p_full, proj_momentum, embed_grad, embed_momentum,
        token_counts.reshape(-1, 1),
    )


def solution(mesh):
    fine = Mesh(mesh.devices.reshape(4, 2, 4, 2, 2), ("y", "zh", "x", "zl", "c"))
    shard, tensor = ("y", "zh", "x"), ("zl", "c")
    rows = P(shard + tensor, None)
    return jax.shard_map(
        per_device,
        mesh=fine,
        in_specs=(
            P(shard, tensor), P(None, shard, tensor), P(None, shard),
            rows, rows, rows, rows, P(shard + tensor),
        ),
        out_specs=(rows, rows),
        check_vma=False,
    )
```

time: 1500 us -> 174 us (0.12)
  waiting for transfers between devices: 917 us -> 33.2 us
  local copies, waits for them, and re-layouts: 212 us -> 6.52 us
  blocking collectives: 252 us -> 74.7 us
  matrix products: 62.1 us -> 0 us
  Pallas kernels: 0 us -> 38.4 us
  other arithmetic: 29 us -> 3.72 us
  between operations: 17.6 us -> 0.72 us
    all_gather x4 -> x0, waiting for transfers between devices: 789 us -> none  [the longest x3 610 us: per_device(): inverses = lax.all_gather(rows_now, ('shard', 'tensor'), axis=0, tiled=True)]
    unnamed x6 -> x0, waiting for transfers between devices: 128 us -> none
    all_to_all x1 -> x2, blocking collectives: 188 us -> 74.7 us  [exchange(): return lax.all_to_all(x, CHIP_AXES, split_axis=0, concat_axis=0, tiled=True)]
    gather x3 -> x0, local copies, waits for them, and re-layouts: 98.7 us -> none  [the longest x1 32.9 us: per_device(): jnp.take(out_grads[0], sampled_rows[0], axis=0)]
    psum x1 -> x0, blocking collectives: 64.2 us -> none  [per_device(): lax.psum((frob_part, trace_part, count_part), ('shard', 'tensor'))]
    dot_general x8 -> x0, matrix products: 62.1 us -> none  [the longest x2 15.9 us: per_device(): product = jnp.einsum('rfk,kfj->rfj', damped, inverses, precision=highest)]
    all_to_all x2 -> x1, local copies, waits for them, and re-layouts: 50.8 us -> 1.37 us  [exchange(): return lax.all_to_all(x, CHIP_AXES, split_axis=0, concat_axis=0, tiled=True)]
    pallas_call x0 -> x4, Pallas kernels: none -> 38.4 us  [the longest x1 27.4 us: per_device(): pl.pallas_call(finish_kernel, out_shape=(jax.ShapeDtypeStruct(proj_moment...]
  transfers between devices with their start and end apart: 5 -> 6, of which waited for: 5 -> 3; matrix products, arithmetic and copies ran while one was open for 4% -> 4% of each run, Pallas kernels for 0% -> 2%
where the time goes in v1:
time: 174 us; the launch traced here: 173 us
  blocking collectives  74.7 us (43%)
  Pallas kernels  38.4 us (22%)
  waiting for transfers between devices  33.2 us (19%)
  starting transfers between devices  15.7 us (9%)
  local copies, waits for them, and re-layouts  6.52 us (4%)
  other arithmetic  3.72 us (2%)
    all_to_all x2, blocking collectives, exchange(): return lax.all_to_all(x, CHIP_AXES, split_axis=0, concat_axis=0, tiled=True)  74.7 us
    pallas_call x1, Pallas kernels, per_device(): pl.pallas_call(finish_kernel, out_shape=(jax.ShapeDtypeStruct(proj_moment...  27.4 us
    all_to_all x1, waiting for transfers between devices, exchange(): return lax.all_to_all(x, CHIP_AXES, split_axis=0, concat_axis=0, tiled=True)  19.9 us
    ppermute x5, waiting for transfers between devices, to_other(): return lax.ppermute(x, axis, [(0, 1), (1, 0)])  13.3 us
    ppermute x5, starting transfers between devices, to_other(): return lax.ppermute(x, axis, [(0, 1), (1, 0)])  10.3 us
    all_to_all x1, starting transfers between devices, exchange(): return lax.all_to_all(x, CHIP_AXES, split_axis=0, concat_axis=0, tiled=True)  5.37 us
    pallas_call x1, Pallas kernels, per_device(): pl.pallas_call(gram_kernel, out_shape=jax.ShapeDtypeStruct((CHIPS, HALF,...  5.11 us
  transfers between devices with their start and end apart: 6, of which 3 were waited for; matrix products, arithmetic and copies ran while one was open for 4% of the time, Pallas kernels for 2%

profile of v1, /device:TPU:1, one launch (start us, length us, event | category | flops | bytes accessed | tf_op | source)
XLA Modules:
  0.0 172.9 jit_solution(8574958108100772010)
XLA Ops:
  0.6 1.3 fusion.2
  1.9 0.0 copy-start
  2.0 2.5 %collective-permute-start.1 = (bf16[3,192,512]{2,1,0:T(8,128)(2,1)S(1)}, bf16[3,192,512]{2,1,0:T(8,128)(2,1)S(1)}, u32[]{:S(2)}, u32[]{:S(2)}) collective-permute-start(bf16[3,192,512]{2,1,0:T(8,128)(2,1)S(1)} %get-tuple-element.4), channel_id=1, source_target_pairs={{0,2},{2,0},{1,3},{3,1},{4,6},{6,4},{5,7},{7,5},{8,10},{10,8},{9,1... | collective-permute-start | bytes 1769480 | tf_op jit(solution)/shard_map/ppermute | solution.py:177
  4.5 1.0 collective-permute-start
  5.5 12.1 %collective-permute-done.1.other_ref = bf16[3,192,512]{2,1,0:T(8,128)(2,1)S(1)} collective-permute-done((bf16[3,192,512]{2,1,0:T(8,128)(2,1)S(1)}, bf16[3,192,512]{2,1,0:T(8,128)(2,1)S(1)}, u32[]{:S(2)}, u32[]{:S(2)}) %collective-permute-start.1) | collective-permute-done | bytes 589856 | tf_op jit(solution)/shard_map/ppermute | solution.py:177
  17.5 0.0 copy-start.1
  17.5 1.3 collective-permute-start.2
  18.8 2.6 %histogram.1.hist_ref = f32[2,16,128]{2,1,0:T(8,128)} custom-call(s32[1]{0:T(128)} %bitcast.2.info, s32[2,8192]{1,0:T(2,128)} %ids_ref.1), custom_call_target="tpu_custom_call" | custom-call | tf_op jit(solution)/shard_map/histogram/pallas_call | solution.py:196
  21.4 0.6 pad_add_fusion.1.info
  22.1 0.0 collective-permute-done.own_c_ref
  22.1 0.0 copy-start.2
  22.1 0.0 collective-permute-done.2.other_c_ref
  22.1 0.0 copy-start.3
  22.1 0.0 copy-done
  22.1 0.0 copy-done.1
  22.1 0.8 copy-done.2
  22.9 0.2 copy-done.3
  23.1 5.1 %gram.1 = f32[64,64,128]{2,1,0:T(8,128)} custom-call(s32[2]{0:T(128)} %pad_add_fusion.1.info, f32[2,16,128]{2,1,0:T(8,128)} %histogram.1.hist_ref, bf16[3,192,512]{2,1,0:T(8,128)(2,1)} %copy-done, bf16[3,192,512]{2,1,0:T(8,128)(2,1)} %copy-done.2, bf16[3,192,512]{2,1,0:T(8,128)(2,1)} %copy-done.1, bf16[3,192,512]{2,1,0:T(8,128)(2,1)} %copy-done.3, ...), custom_call_target="tpu_custom_call" | custom-call | tf_op jit(solution)/shard_map/gram/pallas_call | solution.py:205
  28.2 40.7 %all_to_all.15.in_ref = f32[64,64,128]{2,1,0:T(8,128)} all-to-all(f32[64,64,128]{2,1,0:T(8,128)} %gram.1), channel_id=1, replica_groups=mesh['y'=4,'zh'=2,'x'=4,'zl'=2,'c'=2] {'y','zh','x','zl'}, dimensions={0} | all-to-all | bytes 4194304 | tf_op jit(solution)/shard_map/all_to_all | solution.py:181
  68.9 3.3 %total.1 = f32[64,64,128]{2,1,0:T(8,128)} custom-call(f32[64,64,128]{2,1,0:T(8,128)} %all_to_all.15.in_ref), custom_call_target="tpu_custom_call" | custom-call | tf_op jit(solution)/shard_map/total/pallas_call | solution.py:222
  72.2 0.0 copy-start.4
  72.2 34.0 %all_to_all.16.own_ref = f32[64,64,128]{2,1,0:T(8,128)} all-to-all(f32[64,64,128]{2,1,0:T(8,128)} %total.1), channel_id=1, replica_groups=mesh['y'=4,'zh'=2,'x'=4,'zl'=2,'c'=2] {'y','zh','x','zl'}, dimensions={0} | all-to-all | bytes 4194304 | tf_op jit(solution)/shard_map/all_to_all | solution.py:181
  106.2 0.0 copy-done.4
  106.2 1.3 broadcast_in_dim.10
  107.4 5.4 %all-to-all-start.2 = ((f32[64,6,768]{2,1,0:T(8,128)}), f32[64,6,768]{2,1,0:T(8,128)S(1)}, u32[]{:S(2)}, u32[]{:S(2)}) async-start(f32[64,6,768]{2,1,0:T(8,128)} %broadcast_in_dim.10), calls=%async_computation.2 | async-start | bytes 3145728 | tf_op jit(solution)/shard_map/all_to_all | solution.py:181
  112.8 0.0 copy-start.5
  112.8 2.2 %collective-permute-start.3 = (f32[64,64,128]{2,1,0:T(8,128)}, f32[64,64,128]{2,1,0:T(8,128)}, u32[]{:S(2)}, u32[]{:S(2)}) collective-permute-start(f32[64,64,128]{2,1,0:T(8,128)} %all_to_all.16.own_ref), channel_id=1, source_target_pairs={{0,1},{1,0},{2,3},{3,2},{4,5},{5,4},{6,7},{7,6},{8,9},{9,8},{10,11... | collective-permute-start | bytes 6291464 | tf_op jit(solution)/shard_map/ppermute | solution.py:177
  115.0 19.9 %all-to-all-done.2 = f32[64,6,768]{2,1,0:T(8,128)S(1)} async-done(((f32[64,6,768]{2,1,0:T(8,128)}), f32[64,6,768]{2,1,0:T(8,128)S(1)}, u32[]{:S(2)}, u32[]{:S(2)}) %all-to-all-start.2) | async-done | bytes 1179680 | tf_op jit(solution)/shard_map/all_to_all | solution.py:181
  134.8 1.4 copy.15
  136.2 3.4 %collective-permute-start.4 = (f32[64,6,768]{2,0,1:T(8,128)}, f32[64,6,768]{2,0,1:T(8,128)S(1)}, u32[]{:S(2)}, u32[]{:S(2)}) collective-permute-start(f32[64,6,768]{2,0,1:T(8,128)} %copy.15), channel_id=1, source_target_pairs={{0,1},{1,0},{2,3},{3,2},{4,5},{5,4},{6,7},{7,6},{8,9},{9,8},{10,11... | collective-permute-start | bytes 3538952 | tf_op jit(solution)/shard_map/ppermute | solution.py:177
  139.7 0.0 copy-done.5
  139.7 0.8 reshape.17.count_ref
  140.5 0.6 pad_add_fusion.info
  141.1 1.2 collective-permute-done.4
  142.3 0.8 fusion
  143.2 0.3 pad_maximum_fusion
  143.5 0.4 copy.18
  143.9 1.6 reshape.15.p_ref
  145.5 0.0 collective-permute-done.3.other_ref
  145.6 27.4 %finish.1 = (f32[6,768]{1,0:T(8,128)}, f32[384,768]{1,0:T(8,128)}) custom-call(s32[2]{0:T(128)} %pad_add_fusion.info, f32[64,64,128]{2,1,0:T(8,128)} %all_to_all.16.own_ref, f32[64,64,128]{2,1,0:T(8,128)} %collective-permute-done.3.other_ref, f32[768,768]{1,0:T(8,128)} %reshape.15.p_ref, f32[6,768]{1,0:T(8,128)} %p_mom_ref.1, f32[384,768]{1,0:T(8,128)} %g_ref.1, ...), custom_call_target="tpu_custom_call" | custom-call | tf_op jit(solution)/shard_map/finish/pallas_call | solution.py:233
Async XLA Ops:
  1.9 20.2 %copy-start = (bf16[3,192,512]{2,1,0:T(8,128)(2,1)}, bf16[3,192,512]{2,1,0:T(8,128)(2,1)S(1)}, u32[]{:S(2)}) copy-start(bf16[3,192,512]{2,1,0:T(8,128)(2,1)S(1)} %get-tuple-element.5.own_ref) | copy-start | bytes 1769476
  2.0 15.6 %collective-permute-start.1 = (bf16[3,192,512]{2,1,0:T(8,128)(2,1)S(1)}, bf16[3,192,512]{2,1,0:T(8,128)(2,1)S(1)}, u32[]{:S(2)}, u32[]{:S(2)}) collective-permute-start(bf16[3,192,512]{2,1,0:T(8,128)(2,1)S(1)} %get-tuple-element.4), channel_id=1, source_target_pairs={{0,2},{2,0},{1,3},{3,1},{4,6},{6,4},{5,7},{7,5},{8,10},{10,8},{9,1... | collective-permute-start | bytes 1769480 | tf_op jit(solution)/shard_map/ppermute | solution.py:177
  4.5 17.6 %collective-permute-start = (bf16[3,192,512]{2,1,0:T(8,128)(2,1)S(1)}, bf16[3,192,512]{2,1,0:T(8,128)(2,1)S(1)}, u32[]{:S(2)}, u32[]{:S(2)}) collective-permute-start(bf16[3,192,512]{2,1,0:T(8,128)(2,1)S(1)} %get-tuple-element.5.own_ref), channel_id=1, source_target_pairs={{0,1},{1,0},{2,3},{3,2},{4,5},{5,4},{6,7},{7,6},{8,9},{9,8},{10,11... | collective-permute-start | bytes 1769480 | tf_op jit(solution)/shard_map/ppermute | solution.py:177
  17.5 4.6 %copy-start.1 = (bf16[3,192,512]{2,1,0:T(8,128)(2,1)}, bf16[3,192,512]{2,1,0:T(8,128)(2,1)S(1)}, u32[]{:S(2)}) copy-start(bf16[3,192,512]{2,1,0:T(8,128)(2,1)S(1)} %collective-permute-done.1.other_ref) | copy-start | bytes 1769476
  17.5 4.5 %collective-permute-start.2 = (bf16[3,192,512]{2,1,0:T(8,128)(2,1)S(1)}, bf16[3,192,512]{2,1,0:T(8,128)(2,1)S(1)}, u32[]{:S(2)}, u32[]{:S(2)}) collective-permute-start(bf16[3,192,512]{2,1,0:T(8,128)(2,1)S(1)} %collective-permute-done.1.other_ref), channel_id=1, source_target_pairs={{0,1},{1,0},{2,3},{3,2},{4,5},{5,4},{6,7},{7,6},{8,9},{9,8},{10,11... | collective-permute-start | bytes 1769480 | tf_op jit(solution)/shard_map/ppermute | solution.py:177
  22.1 0.8 copy-start.2
  22.1 1.0 copy-start.3
  72.2 34.0 %copy-start.4 = (f32[6,768]{1,0:T(8,128)S(1)}, f32[6,768]{1,0:T(8,128)}, u32[]{:S(2)}) copy-start(f32[6,768]{1,0:T(8,128)} %param.11) | copy-start | bytes 55300
  107.4 27.4 %all-to-all-start.2 = ((f32[64,6,768]{2,1,0:T(8,128)}), f32[64,6,768]{2,1,0:T(8,128)S(1)}, u32[]{:S(2)}, u32[]{:S(2)}) async-start(f32[64,6,768]{2,1,0:T(8,128)} %broadcast_in_dim.10), calls=%async_computation.2 | async-start | bytes 3145728 | tf_op jit(solution)/shard_map/all_to_all | solution.py:181
  112.8 26.9 %copy-start.5 = (s32[384]{0:T(512)S(1)}, s32[384]{0:T(512)}, u32[]{:S(2)}) copy-start(s32[384]{0:T(512)} %param.15) | copy-start | bytes 4612
  112.8 32.7 %collective-permute-start.3 = (f32[64,64,128]{2,1,0:T(8,128)}, f32[64,64,128]{2,1,0:T(8,128)}, u32[]{:S(2)}, u32[]{:S(2)}) collective-permute-start(f32[64,64,128]{2,1,0:T(8,128)} %all_to_all.16.own_ref), channel_id=1, source_target_pairs={{0,1},{1,0},{2,3},{3,2},{4,5},{5,4},{6,7},{7,6},{8,9},{9,8},{10,11... | collective-permute-start | bytes 6291464 | tf_op jit(solution)/shard_map/ppermute | solution.py:177
  136.2 6.1 %collective-permute-start.4 = (f32[64,6,768]{2,0,1:T(8,128)}, f32[64,6,768]{2,0,1:T(8,128)S(1)}, u32[]{:S(2)}, u32[]{:S(2)}) collective-permute-start(f32[64,6,768]{2,0,1:T(8,128)} %copy.15), channel_id=1, source_target_pairs={{0,1},{1,0},{2,3},{3,2},{4,5},{5,4},{6,7},{7,6},{8,9},{9,8},{10,11... | collective-permute-start | bytes 3538952 | tf_op jit(solution)/shard_map/ppermute | solution.py:177

commit v2 on v1

--- a/solution.py
+++ b/solution.py
@@ -66,11 +66,23 @@
         out_ref[k] = total
 
 
+def swap_halves(x):
+    return pltpu.roll(x, HALF, 1)
+
+
+def pair_up(x, lane):
+    hi, lo = split(x)
+    return jnp.where(lane < HALF, hi.astype(f32), lo.astype(f32))
+
+
 def gram_kernel(info, hist_ref, own_ref, own_c_ref, other_ref, other_c_ref, count_ref, out_ref, x_ref):
     zl, core = info[0], info[1]
     places = [2 * zl + core, 2 * zl + 1 - core, 2 * (1 - zl) + core, 2 * (1 - zl) + 1 - core]
-    tokens = jnp.sum(count_ref[...].astype(f32), keepdims=True).reshape(1, 1)
-    out_ref[CHIPS - 1] = jnp.broadcast_to(tokens, (HALF, BLK)).astype(out_ref.dtype)
+    on_diagonal = (
+        lax.broadcasted_iota(jnp.int32, (HALF, BLK), 1)
+        == lax.broadcasted_iota(jnp.int32, (HALF, BLK), 0) + core * HALF
+    )
+    exact = []
     for f in range(3):
         for place, ref in zip(places, (own_ref, own_c_ref, other_ref, other_c_ref)):
             x_ref[pl.ds(pl.multiple_of(place * 192, 192), 192), :] = ref[f]
@@ -84,64 +96,84 @@
         gram = nt_dot(hi, x) + nt_dot(lo, x)
         for b, (g, i, j) in enumerate(BLOCKS):
             if g == f:
-                out_ref[b] = gram[i * HALF : (i + 1) * HALF, j * BLK : (j + 1) * BLK].astype(out_ref.dtype)
-
-
-def total_kernel(in_ref, out_ref):
+                block = gram[i * HALF : (i + 1) * HALF, j * BLK : (j + 1) * BLK]
+                out_ref[b] = block.astype(bf16)
+                if i == j:
+                    exact.append(jnp.sum(jnp.where(on_diagonal, block, 0.0), axis=0, keepdims=True))
+    tokens = jnp.sum(count_ref[...].astype(f32), keepdims=True).reshape(1, 1)
+    lane = lax.broadcasted_iota(jnp.int32, (1, BLK), 1)
+    exact.append(jnp.where(lane < HALF, tokens, 0.0))
+    exact = jnp.concatenate(exact + [jnp.zeros((HALF - len(exact), BLK), f32)], axis=0)
+    exact = exact + swap_halves(exact)
+    lane = lax.broadcasted_iota(jnp.int32, (HALF, BLK), 1)
+    out_ref[CHIPS - 1] = pair_up(exact, lane).astype(bf16)
+
+
+def total_kernel(info, in_ref, out_ref):
     total = jnp.sum(in_ref[...].astype(f32), axis=0) * (1.0 / SAMPLES)
+    lane = lax.broadcasted_iota(jnp.int32, (HALF, BLK), 1)
+    exact = pair_up(total + swap_halves(total), lane)
+    total = jnp.where(info[0] == CHIPS - 1, exact, total).astype(bf16)
     for s in range(CHIPS):
-        out_ref[s] = total.astype(out_ref.dtype)
-
-
-def step(y, start, hi_ref, lo_ref):
-    y_hi, y_lo = split(y)
-    hi, lo = hi_ref[...], lo_ref[...]
-    return start + y - (nn_dot(y_hi, hi) + nn_dot(y_lo, hi) + nn_dot(y_hi, lo))
+        out_ref[s] = total
+
+
+def step(y, start, keep, scale, r_ref):
+    hi, lo = split(y)
+    return start + y * keep - scale * (nn_dot(hi, r_ref[...]) + nn_dot(lo, r_ref[...]))
+
+
+def thin_step(y, start, keep, scale, r_ref):
+    hi, lo = split(y)
+    both = nn_dot(jnp.concatenate([hi, lo], axis=0), r_ref[...])
+    return start + y * keep - scale * (both[:8] + both[8:])
 
 
 def finish_kernel(
     info, own_ref, other_ref, p_ref, p_mom_ref, g_ref, e_mom_ref, count_ref,
-    p_out_ref, e_out_ref, full_ref, hi_ref, lo_ref, y_ref,
+    p_out_ref, e_out_ref, r_ref, y_ref,
 ):
     core, flat = info[0], info[1]
-    rows = lax.broadcasted_iota(jnp.int32, (BLK, BLK), 0)
-    cols = lax.broadcasted_iota(jnp.int32, (BLK, BLK), 1)
-    diagonal = rows == cols
-    zero = jnp.zeros((BLK, BLK), f32)
-    squares = [zero, zero, zero]
-    traces = [zero, zero, zero]
+    row = lax.broadcasted_iota(jnp.int32, (HALF, BLK), 0)
+    col = lax.broadcasted_iota(jnp.int32, (HALF, BLK), 1)
+    squares = [jnp.zeros((HALF, BLK), f32) for _ in range(3)]
+    for part, ref in ((core, own_ref), (1 - core, other_ref)):
+        off_diagonal = col != row + part * HALF
+        for b, (f, i, j) in enumerate(BLOCKS):
+            start = pl.multiple_of(i * BLK + part * HALF, HALF)
+            block = ref[b]
+            wide = block.astype(f32)
+            if i == j:
+                wide = jnp.where(off_diagonal, wide, 0.0)
+                block = wide.astype(bf16)
+                squares[f] = squares[f] + wide * wide
+            else:
+                squares[f] = squares[f] + 2.0 * (wide * wide)
+            r_ref[f, pl.ds(start, HALF), j * BLK : (j + 1) * BLK] = block
     for b, (f, i, j) in enumerate(BLOCKS):
-        for part, ref in ((core, own_ref), (1 - core, other_ref)):
-            start = pl.multiple_of(i * BLK + part * HALF, HALF)
-            full_ref[f, pl.ds(start, HALF), j * BLK : (j + 1) * BLK] = ref[b].astype(f32)
-        block = full_ref[f, i * BLK : (i + 1) * BLK, j * BLK : (j + 1) * BLK]
-        if i == j:
-            squares[f] = squares[f] + block * block
-            traces[f] = traces[f] + jnp.where(diagonal, block, 0.0)
-        else:
-            squares[f] = squares[f] + 2.0 * block * block
-    squares = [jnp.sum(s, keepdims=True) for s in squares]
-    traces = [jnp.sum(t, keepdims=True) for t in traces]
-    tokens = (own_ref[CHIPS - 1][0:1, 0:1] + other_ref[CHIPS - 1][0:1, 0:1]) * float(SAMPLES)
+        if i != j:
+            block = r_ref[f, i * BLK : (i + 1) * BLK, j * BLK : (j + 1) * BLK]
+            r_ref[f, j * BLK : (j + 1) * BLK, i * BLK : (i + 1) * BLK] = block.T
+
+    own = own_ref[CHIPS - 1].astype(f32)
+    other = other_ref[CHIPS - 1].astype(f32)
+    own = own + swap_halves(own)
+    other = other + swap_halves(other)
+    exact = jnp.where((col < HALF) == (core == 0), own, other)
+    tokens = (own + other)[18:19, 0:1] * float(SAMPLES)
+    diagonals = [
+        jnp.concatenate([exact[f * NB + i : f * NB + i + 1, :] for i in range(NB)], axis=1) for f in range(3)
+    ]
+    traces = [jnp.sum(d, keepdims=True) for d in diagonals]
+    squares = [jnp.sum(s, keepdims=True) + jnp.sum(d * d, keepdims=True) for s, d in zip(squares, diagonals)]
     ratio = jnp.sqrt(traces[0] / traces[1])
     embed_ratio = jnp.sqrt(tokens / count_scale / VOCAB / (traces[2] / D))
     shifts = [damping_root * ratio, damping_root / ratio, damping_root / embed_ratio]
-    scales = []
+    scales, keeps = [], []
     for f in range(3):
         q = squares[f] + 2.0 * shifts[f] * traces[f] + D * shifts[f] * shifts[f]
         scales.append(1.0 / jnp.sqrt(q))
-    for b, (f, i, j) in enumerate(BLOCKS):
-        block = full_ref[f, i * BLK : (i + 1) * BLK, j * BLK : (j + 1) * BLK]
-        if i == j:
-            block = block + jnp.where(diagonal, shifts[f], 0.0)
-        block = block * scales[f]
-        hi, lo = split(block)
-        hi_ref[f, i * BLK : (i + 1) * BLK, j * BLK : (j + 1) * BLK] = hi
-        lo_ref[f, i * BLK : (i + 1) * BLK, j * BLK : (j + 1) * BLK] = lo
-        if i != j:
-            hi, lo = split(block.T)
-            hi_ref[f, j * BLK : (j + 1) * BLK, i * BLK : (i + 1) * BLK] = hi
-            lo_ref[f, j * BLK : (j + 1) * BLK, i * BLK : (i + 1) * BLK] = lo
+        keeps.append(1.0 - scales[f] * (diagonals[f] + shifts[f]))
 
     half = 192
     row = lax.broadcasted_iota(jnp.int32, (8, D), 0)
@@ -150,8 +182,8 @@
 
     def first(_, carry):
         a, y = carry
-        a = step(a, unit, hi_ref.at[0], lo_ref.at[0])
-        y = step(y, g_ref[0:half, :], hi_ref.at[2], lo_ref.at[2])
+        a = thin_step(a, unit, keeps[0], scales[0], r_ref.at[0])
+        y = step(y, g_ref[0:half, :], keeps[2], scales[2], r_ref.at[2])
         return a, y
 
     a, y = lax.fori_loop(0, STEPS, first, (unit, g_ref[0:half, :]))
@@ -162,8 +194,8 @@
 
     def second(_, carry):
         a, y = carry
-        a = step(a, mixed, hi_ref.at[1], lo_ref.at[1])
-        y = step(y, g_ref[half:, :], hi_ref.at[2], lo_ref.at[2])
+        a = thin_step(a, mixed, keeps[1], scales[1], r_ref.at[1])
+        y = step(y, g_ref[half:, :], keeps[2], scales[2], r_ref.at[2])
         return a, y
 
     a, y = lax.fori_loop(0, STEPS, second, (mixed, g_ref[half:, :]))
@@ -204,7 +236,7 @@
 
     parts = pl.pallas_call(
         gram_kernel,
-        out_shape=jax.ShapeDtypeStruct((CHIPS, HALF, BLK), f32),
+        out_shape=jax.ShapeDtypeStruct((CHIPS, HALF, BLK), bf16),
         in_specs=[smem()] + [vmem()] * 6,
         out_specs=vmem(),
         scratch_shapes=[pltpu.VMEM((D, 512), bf16)],
@@ -212,21 +244,21 @@
         name="gram",
     )(jnp.stack([zl, core]), hist, keep, keep_c, other, other_c, token_counts.reshape(3, BLK))
 
-    rows = proj_grad.shape[0]
     p_own = exchange(jnp.broadcast_to(proj_grad[None], (CHIPS,) + proj_grad.shape))
     p_other = to_other(p_own, "c")
+    parts, p_own, p_other = lax.optimization_barrier((parts, p_own, p_other))
+    arrived = exchange(parts)
     p_pair = jnp.stack([jnp.where(core == 0, p_own, p_other), jnp.where(core == 0, p_other, p_own)], axis=1)
     p_full = p_pair.reshape(D, D)
 
-    arrived = exchange(parts)
     spread = pl.pallas_call(
         total_kernel,
-        out_shape=jax.ShapeDtypeStruct((CHIPS, HALF, BLK), f32),
-        in_specs=[vmem()],
+        out_shape=jax.ShapeDtypeStruct((CHIPS, HALF, BLK), bf16),
+        in_specs=[smem(), vmem()],
         out_specs=vmem(),
         compiler_params=params(),
         name="total",
-    )(arrived)
+    )(jnp.stack([chip]), arrived)
     own_blocks = exchange(spread)
     other_blocks = to_other(own_blocks, "c")
 
@@ -239,8 +271,6 @@
         in_specs=[smem()] + [vmem()] * 7,
         out_specs=(vmem(), vmem()),
         scratch_shapes=[
-            pltpu.VMEM((3, D, D), f32),
-            pltpu.VMEM((3, D, D), bf16),
             pltpu.VMEM((3, D, D), bf16),
             pltpu.VMEM((384, D), f32),
         ],

time: 174 us -> 137 us (0.79)
  blocking collectives: 74.7 us -> 23.1 us
  starting transfers between devices: 15.7 us -> 27.5 us
  waiting for transfers between devices: 33.2 us -> 44.7 us
  Pallas kernels: 38.4 us -> 28.3 us
  local copies, waits for them, and re-layouts: 6.52 us -> 8.27 us
    all_to_all x2 -> x1, blocking collectives: 74.7 us -> 23.1 us  [exchange(): return lax.all_to_all(x, CHIP_AXES, split_axis=0, concat_axis=0, tiled=True)]
    all_to_all x1 -> x2, waiting for transfers between devices: 19.9 us -> 39.7 us  [exchange(): return lax.all_to_all(x, CHIP_AXES, split_axis=0, concat_axis=0, tiled=True)]
    all_to_all x1 -> x2, starting transfers between devices: 5.37 us -> 21.2 us  [exchange(): return lax.all_to_all(x, CHIP_AXES, split_axis=0, concat_axis=0, tiled=True)]
    pallas_call x1, Pallas kernels: 27.4 us -> 18.3 us  [per_device(): pl.pallas_call(finish_kernel, out_shape=(jax.ShapeDtypeStruct(proj_moment...]
    ppermute x5, waiting for transfers between devices: 13.3 us -> 5.09 us  [to_other(): return lax.ppermute(x, axis, [(0, 1), (1, 0)])]
    ppermute x5, starting transfers between devices: 10.3 us -> 6.29 us  [to_other(): return lax.ppermute(x, axis, [(0, 1), (1, 0)])]
  transfers between devices with their start and end apart: 6 -> 7, of which waited for: 3 -> 3; matrix products, arithmetic and copies ran while one was open for 4% -> 6% of each run, Pallas kernels for 2% -> 6%
where the time goes in v2:
time: 137 us; the launch traced here: 136 us
  waiting for transfers between devices  44.7 us (33%)
  Pallas kernels  28.3 us (21%)
  starting transfers between devices  27.5 us (20%)
  blocking collectives  23.1 us (17%)
  local copies, waits for them, and re-layouts  8.27 us (6%)
  other arithmetic  3.37 us (2%)
    all_to_all x2, waiting for transfers between devices, exchange(): return lax.all_to_all(x, CHIP_AXES, split_axis=0, concat_axis=0, tiled=True)  39.7 us
    all_to_all x1, blocking collectives, exchange(): return lax.all_to_all(x, CHIP_AXES, split_axis=0, concat_axis=0, tiled=True)  23.1 us
    all_to_all x2, starting transfers between devices, exchange(): return lax.all_to_all(x, CHIP_AXES, split_axis=0, concat_axis=0, tiled=True)  21.2 us
    pallas_call x1, Pallas kernels, per_device(): pl.pallas_call(finish_kernel, out_shape=(jax.ShapeDtypeStruct(proj_moment...  18.3 us
    ppermute x5, starting transfers between devices, to_other(): return lax.ppermute(x, axis, [(0, 1), (1, 0)])  6.29 us
    ppermute x5, waiting for transfers between devices, to_other(): return lax.ppermute(x, axis, [(0, 1), (1, 0)])  5.09 us
    pallas_call x1, Pallas kernels, per_device(): pl.pallas_call(gram_kernel, out_shape=jax.ShapeDtypeStruct((CHIPS, HALF,...  4.85 us
  transfers between devices with their start and end apart: 7, of which 3 were waited for; matrix products, arithmetic and copies ran while one was open for 6% of the time, Pallas kernels for 6%

profile of v2, /device:TPU:1, one launch (start us, length us, event | category | flops | bytes accessed | tf_op | source)
XLA Modules:
  0.0 136.0 jit_solution(1891603952242363254)
XLA Ops:
  0.6 2.0 %broadcast_in_dim.10 = f32[64,6,768]{2,1,0:T(8,128)} broadcast(f32[6,768]{1,0:T(8,128)} %param.11), dimensions={1,2} | broadcast | bytes 1198080 | tf_op jit(solution)/shard_map/broadcast_in_dim | solution.py:247
  2.6 0.0 copy-start.4
  2.6 0.0 copy-start.5
  2.6 12.1 %all-to-all-start = ((f32[64,6,768]{2,1,0:T(8,128)}), f32[64,6,768]{2,1,0:T(8,128)S(1)}, u32[]{:S(2)}, u32[]{:S(2)}) async-start(f32[64,6,768]{2,1,0:T(8,128)} %broadcast_in_dim.10), calls=%async_computation | async-start | bytes 3145728 | tf_op jit(solution)/shard_map/all_to_all | solution.py:213
  14.8 0.0 copy-done.4
  14.8 0.0 copy-done.5
  14.8 0.9 fusion.2
  15.7 0.0 copy-start.1
  15.7 1.0 collective-permute-start.1
  16.7 21.2 %all-to-all-done = f32[64,6,768]{2,1,0:T(8,128)S(1)} async-done(((f32[64,6,768]{2,1,0:T(8,128)}), f32[64,6,768]{2,1,0:T(8,128)S(1)}, u32[]{:S(2)}, u32[]{:S(2)}) %all-to-all-start) | async-done | bytes 1179680 | tf_op jit(solution)/shard_map/all_to_all | solution.py:213
  37.9 1.4 %copy.15 = f32[64,6,768]{2,0,1:T(8,128)} copy(f32[64,6,768]{2,1,0:T(8,128)S(1)} %all-to-all-done) | data formatting | bytes 2359296 | tf_op jit(solution)/shard_map/all_to_all | solution.py:213
  39.3 2.2 %collective-permute-start.3 = (f32[64,6,768]{2,0,1:T(8,128)}, f32[64,6,768]{2,0,1:T(8,128)S(1)}, u32[]{:S(2)}, u32[]{:S(2)}) collective-permute-start(f32[64,6,768]{2,0,1:T(8,128)} %copy.15), channel_id=1, source_target_pairs={{0,1},{1,0},{2,3},{3,2},{4,5},{5,4},{6,7},{7,6},{8,9},{9,8},{10,11... | collective-permute-start | bytes 3538952 | tf_op jit(solution)/shard_map/ppermute | solution.py:209
  41.5 0.0 collective-permute-start
  41.5 5.1 %collective-permute-done.1.other_ref = bf16[3,192,512]{2,1,0:T(8,128)(2,1)} collective-permute-done((bf16[3,192,512]{2,1,0:T(8,128)(2,1)}, bf16[3,192,512]{2,1,0:T(8,128)(2,1)}, u32[]{:S(2)}, u32[]{:S(2)}) %collective-permute-start.1) | collective-permute-done | bytes 589856 | tf_op jit(solution)/shard_map/ppermute | solution.py:209
  46.6 0.9 collective-permute-start.2
  47.5 2.6 %histogram.1.hist_ref = f32[2,16,128]{2,1,0:T(8,128)} custom-call(s32[1]{0:T(128)} %bitcast.3.info, s32[2,8192]{1,0:T(2,128)} %ids_ref.1), custom_call_target="tpu_custom_call" | custom-call | tf_op jit(solution)/shard_map/histogram/pallas_call | solution.py:228
  50.1 0.7 pad_add_fusion.1.info
  50.8 0.0 collective-permute-done.own_c_ref
  50.8 0.0 collective-permute-done.2.other_c_ref
  50.8 0.0 copy-done.1
  50.8 4.8 %gram.1 = bf16[64,64,128]{2,1,0:T(8,128)(2,1)} custom-call(s32[2]{0:T(128)} %pad_add_fusion.1.info, f32[2,16,128]{2,1,0:T(8,128)} %histogram.1.hist_ref, bf16[3,192,512]{2,1,0:T(8,128)(2,1)} %copy-done.1, bf16[3,192,512]{2,1,0:T(8,128)(2,1)} %collective-permute-done.own_c_ref, bf16[3,192,512]{2,1,0:T(8,128)(2,1)} %collective-permute-done.1.other_ref, ...), custom_call_target="tpu_custom_call" | custom-call | tf_op jit(solution)/shard_map/gram/pallas_call | solution.py:237
  55.6 0.0 collective-permute-done.3
  55.6 0.0 copy-start.2
  55.6 1.0 copy-done.2
  56.6 9.1 %all-to-all-start.1 = ((bf16[64,64,128]{2,1,0:T(8,128)(2,1)}), bf16[64,64,128]{2,1,0:T(8,128)(2,1)S(1)}, u32[]{:S(2)}, u32[]{:S(2)}) async-start(bf16[64,64,128]{2,1,0:T(8,128)(2,1)} %gram.1), calls=%async_computation.1 | async-start | bytes 2097152 | tf_op jit(solution)/shard_map/all_to_all | solution.py:213
  65.8 18.4 %all-to-all-done.1.in_ref = bf16[64,64,128]{2,1,0:T(8,128)(2,1)S(1)} async-done(((bf16[64,64,128]{2,1,0:T(8,128)(2,1)}), bf16[64,64,128]{2,1,0:T(8,128)(2,1)S(1)}, u32[]{:S(2)}, u32[]{:S(2)}) %all-to-all-start.1) | async-done | bytes 1048608 | tf_op jit(solution)/shard_map/all_to_all | solution.py:213
  84.2 0.0 copy-start
  84.2 1.0 copy-done
  85.2 2.5 %total.1 = bf16[64,64,128]{2,1,0:T(8,128)(2,1)} custom-call(s32[1]{0:T(128)} %bitcast.2.info, bf16[64,64,128]{2,1,0:T(8,128)(2,1)} %copy-done), custom_call_target="tpu_custom_call" | custom-call | tf_op jit(solution)/shard_map/total/pallas_call | solution.py:254
  87.8 0.0 copy-start.6
  87.8 0.0 copy-start.3
  87.8 23.1 %all_to_all.15.own_ref = bf16[64,64,128]{2,1,0:T(8,128)(2,1)} all-to-all(bf16[64,64,128]{2,1,0:T(8,128)(2,1)} %total.1), channel_id=1, replica_groups=mesh['y'=4,'zh'=2,'x'=4,'zl'=2,'c'=2] {'y','zh','x','zl'}, dimensions={0} | all-to-all | bytes 2097152 | tf_op jit(solution)/shard_map/all_to_all | solution.py:213
  110.9 2.2 %collective-permute-start.4 = (bf16[64,64,128]{2,1,0:T(8,128)(2,1)}, bf16[64,64,128]{2,1,0:T(8,128)(2,1)}, u32[]{:S(2)}, u32[]{:S(2)}) collective-permute-start(bf16[64,64,128]{2,1,0:T(8,128)(2,1)} %all_to_all.15.own_ref), channel_id=1, source_target_pairs={{0,1},{1,0},{2,3},{3,2},{4,5},{5,4},{6,7},{7,6},{8,9},{9,8},{10,11... | collective-permute-start | bytes 3145736 | tf_op jit(solution)/shard_map/ppermute | solution.py:209
  113.1 0.0 copy-done.6
  113.1 0.8 reshape.17.count_ref
  113.9 0.7 pad_add_fusion.info
  114.5 0.0 copy-done.3
  114.5 0.8 fusion
  115.3 0.3 pad_maximum_fusion
  115.6 0.4 copy.18
  116.1 1.6 %reshape.15.p_ref = f32[768,768]{1,0:T(8,128)} reshape(f32[64,2,6,768]{3,2,1,0:T(8,128)S(1)} %copy.18) | data formatting | bytes 4718592 | tf_op jit(solution)/shard_map/reshape | solution.py:252
  117.7 0.0 collective-permute-done.4.other_ref
  117.7 18.3 %finish.1 = (f32[6,768]{1,0:T(8,128)}, f32[384,768]{1,0:T(8,128)}) custom-call(s32[2]{0:T(128)} %pad_add_fusion.info, bf16[64,64,128]{2,1,0:T(8,128)(2,1)} %all_to_all.15.own_ref, bf16[64,64,128]{2,1,0:T(8,128)(2,1)} %collective-permute-done.4.other_ref, f32[768,768]{1,0:T(8,128)} %reshape.15.p_ref, f32[6,768]{1,0:T(8,128)} %p_mom_ref.1, f32[384,768]{1,0:T(8,128)} %g_ref.1, ...), custom_call_target="tpu_custom_call" | custom-call | tf_op jit(solution)/shard_map/finish/pallas_call | solution.py:265
Async XLA Ops:
  2.6 12.1 %copy-start.4 = (bf16[2,1024,192]{1,2,0:T(8,128)(2,1)S(1)}, bf16[2,1024,192]{1,2,0:T(8,128)(2,1)}, u32[]{:S(2)}) copy-start(bf16[2,1024,192]{1,2,0:T(8,128)(2,1)} %param.9) | copy-start | bytes 2359300
  2.6 12.1 %copy-start.5 = (bf16[1024,192]{0,1:T(8,128)(2,1)S(1)}, bf16[1024,192]{0,1:T(8,128)(2,1)}, u32[]{:S(2)}) copy-start(bf16[1024,192]{0,1:T(8,128)(2,1)} %param.8) | copy-start | bytes 1179652
  2.6 35.3 %all-to-all-start = ((f32[64,6,768]{2,1,0:T(8,128)}), f32[64,6,768]{2,1,0:T(8,128)S(1)}, u32[]{:S(2)}, u32[]{:S(2)}) async-start(f32[64,6,768]{2,1,0:T(8,128)} %broadcast_in_dim.10), calls=%async_computation | async-start | bytes 3145728 | tf_op jit(solution)/shard_map/all_to_all | solution.py:213
  15.7 35.0 %copy-start.1 = (bf16[3,192,512]{2,1,0:T(8,128)(2,1)}, bf16[3,192,512]{2,1,0:T(8,128)(2,1)S(1)}, u32[]{:S(2)}) copy-start(bf16[3,192,512]{2,1,0:T(8,128)(2,1)S(1)} %get-tuple-element.11.own_ref) | copy-start | bytes 1769476
  15.7 30.9 %collective-permute-start.1 = (bf16[3,192,512]{2,1,0:T(8,128)(2,1)}, bf16[3,192,512]{2,1,0:T(8,128)(2,1)}, u32[]{:S(2)}, u32[]{:S(2)}) collective-permute-start(bf16[3,192,512]{2,1,0:T(8,128)(2,1)} %get-tuple-element.10), channel_id=1, source_target_pairs={{0,2},{2,0},{1,3},{3,1},{4,6},{6,4},{5,7},{7,5},{8,10},{10,8},{9,1... | collective-permute-start | bytes 1769480 | tf_op jit(solution)/shard_map/ppermute | solution.py:209
  39.3 16.3 %collective-permute-start.3 = (f32[64,6,768]{2,0,1:T(8,128)}, f32[64,6,768]{2,0,1:T(8,128)S(1)}, u32[]{:S(2)}, u32[]{:S(2)}) collective-permute-start(f32[64,6,768]{2,0,1:T(8,128)} %copy.15), channel_id=1, source_target_pairs={{0,1},{1,0},{2,3},{3,2},{4,5},{5,4},{6,7},{7,6},{8,9},{9,8},{10,11... | collective-permute-start | bytes 3538952 | tf_op jit(solution)/shard_map/ppermute | solution.py:209
  41.5 9.2 %collective-permute-start = (bf16[3,192,512]{2,1,0:T(8,128)(2,1)S(1)}, bf16[3,192,512]{2,1,0:T(8,128)(2,1)}, u32[]{:S(2)}, u32[]{:S(2)}) collective-permute-start(bf16[3,192,512]{2,1,0:T(8,128)(2,1)S(1)} %get-tuple-element.11.own_ref), channel_id=1, source_target_pairs={{0,1},{1,0},{2,3},{3,2},{4,5},{5,4},{6,7},{7,6},{8,9},{9,8},{10,11... | collective-permute-start | bytes 1769480 | tf_op jit(solution)/shard_map/ppermute | solution.py:209
  46.6 4.2 %collective-permute-start.2 = (bf16[3,192,512]{2,1,0:T(8,128)(2,1)}, bf16[3,192,512]{2,1,0:T(8,128)(2,1)}, u32[]{:S(2)}, u32[]{:S(2)}) collective-permute-start(bf16[3,192,512]{2,1,0:T(8,128)(2,1)} %collective-permute-done.1.other_ref), channel_id=1, source_target_pairs={{0,1},{1,0},{2,3},{3,2},{4,5},{5,4},{6,7},{7,6},{8,9},{9,8},{10,11... | collective-permute-start | bytes 1769480 | tf_op jit(solution)/shard_map/ppermute | solution.py:209
  55.6 1.0 copy-start.2
  56.6 27.6 %all-to-all-start.1 = ((bf16[64,64,128]{2,1,0:T(8,128)(2,1)}), bf16[64,64,128]{2,1,0:T(8,128)(2,1)S(1)}, u32[]{:S(2)}, u32[]{:S(2)}) async-start(bf16[64,64,128]{2,1,0:T(8,128)(2,1)} %gram.1), calls=%async_computation.1 | async-start | bytes 2097152 | tf_op jit(solution)/shard_map/all_to_all | solution.py:213
  84.2 1.0 copy-start
  87.8 25.3 %copy-start.6 = (s32[384]{0:T(512)S(1)}, s32[384]{0:T(512)}, u32[]{:S(2)}) copy-start(s32[384]{0:T(512)} %param.15) | copy-start | bytes 4612
  87.8 26.8 %copy-start.3 = (f32[64,6,768]{2,0,1:T(8,128)S(1)}, f32[64,6,768]{2,0,1:T(8,128)}, u32[]{:S(2)}) copy-start(f32[64,6,768]{2,0,1:T(8,128)} %copy-done.2) | copy-start | bytes 3538948
  110.9 6.9 %collective-permute-start.4 = (bf16[64,64,128]{2,1,0:T(8,128)(2,1)}, bf16[64,64,128]{2,1,0:T(8,128)(2,1)}, u32[]{:S(2)}, u32[]{:S(2)}) collective-permute-start(bf16[64,64,128]{2,1,0:T(8,128)(2,1)} %all_to_all.15.own_ref), channel_id=1, source_target_pairs={{0,1},{1,0},{2,3},{3,2},{4,5},{5,4},{6,7},{7,6},{8,9},{9,8},{10,11... | collective-permute-start | bytes 3145736 | tf_op jit(solution)/shard_map/ppermute | solution.py:209

commit v3 on v2

--- a/solution.py
+++ b/solution.py
@@ -221,6 +221,7 @@
     features = jnp.concatenate([acts.T[None], jnp.transpose(out_grads, (0, 2, 1))], axis=0)
     keep = lax.dynamic_slice_in_dim(features, zl * 512, 512, 2)
     send = lax.dynamic_slice_in_dim(features, (1 - zl) * 512, 512, 2)
+    send, keep, p_rows = lax.optimization_barrier((send, keep, proj_grad))
     other = to_other(send, "zl")
     keep_c = to_other(keep, "c")
     other_c = to_other(other, "c")
@@ -244,10 +245,10 @@
         name="gram",
     )(jnp.stack([zl, core]), hist, keep, keep_c, other, other_c, token_counts.reshape(3, BLK))
 
-    p_own = exchange(jnp.broadcast_to(proj_grad[None], (CHIPS,) + proj_grad.shape))
+    p_own = exchange(jnp.broadcast_to(p_rows[None], (CHIPS,) + proj_grad.shape))
+    parts, p_own = lax.optimization_barrier((parts, p_own))
+    arrived = exchange(parts)
     p_other = to_other(p_own, "c")
-    parts, p_own, p_other = lax.optimization_barrier((parts, p_own, p_other))
-    arrived = exchange(parts)
     p_pair = jnp.stack([jnp.where(core == 0, p_own, p_other), jnp.where(core == 0, p_other, p_own)], axis=1)
     p_full = p_pair.reshape(D, D)
 

time: 137 us -> 126 us (0.920)
  blocking collectives: 23.1 us -> 0 us
  starting transfers between devices: 27.5 us -> 40.4 us
    all_to_all x1 -> x0, blocking collectives: 23.1 us -> none  [exchange(): return lax.all_to_all(x, CHIP_AXES, split_axis=0, concat_axis=0, tiled=True)]
    all_to_all x2 -> x3, starting transfers between devices: 21.2 us -> 31.7 us  [exchange(): return lax.all_to_all(x, CHIP_AXES, split_axis=0, concat_axis=0, tiled=True)]
    ppermute x5, waiting for transfers between devices: 5.09 us -> 0.01 us  [to_other(): return lax.ppermute(x, axis, [(0, 1), (1, 0)])]
    all_to_all x2 -> x3, waiting for transfers between devices: 39.7 us -> 44.7 us  [exchange(): return lax.all_to_all(x, CHIP_AXES, split_axis=0, concat_axis=0, tiled=True)]
    ppermute x5, starting transfers between devices: 6.29 us -> 8.76 us  [to_other(): return lax.ppermute(x, axis, [(0, 1), (1, 0)])]
    optimization_barrier x0 -> x1, local copies, waits for them, and re-layouts: none -> 1.38 us  [per_device(): parts, p_own = lax.optimization_barrier((parts, p_own))]
    all_to_all x1 -> x0, local copies, waits for them, and re-layouts: 1.37 us -> none  [exchange(): return lax.all_to_all(x, CHIP_AXES, split_axis=0, concat_axis=0, tiled=True)]
  transfers between devices with their start and end apart: 7 -> 8, of which waited for: 3 -> 3; matrix products, arithmetic and copies ran while one was open for 6% -> 6% of each run, Pallas kernels for 6% -> 6%
where the time goes in v3:
time: 126 us
  waiting for transfers between devices  44.7 us (35%)
  starting transfers between devices  40.4 us (32%)
  Pallas kernels  28.3 us (22%)
  local copies, waits for them, and re-layouts  7.29 us (6%)
  other arithmetic  4.45 us (4%)
    all_to_all x3, waiting for transfers between devices, exchange(): return lax.all_to_all(x, CHIP_AXES, split_axis=0, concat_axis=0, tiled=True)  44.7 us
    all_to_all x3, starting transfers between devices, exchange(): return lax.all_to_all(x, CHIP_AXES, split_axis=0, concat_axis=0, tiled=True)  31.7 us
    pallas_call x1, Pallas kernels, per_device(): pl.pallas_call(finish_kernel, out_shape=(jax.ShapeDtypeStruct(proj_moment...  18.3 us
    ppermute x5, starting transfers between devices, to_other(): return lax.ppermute(x, axis, [(0, 1), (1, 0)])  8.76 us
    pallas_call x1, Pallas kernels, per_device(): pl.pallas_call(gram_kernel, out_shape=jax.ShapeDtypeStruct((CHIPS, HALF,...  4.83 us
    pallas_call x1, Pallas kernels, per_device(): pl.pallas_call(histogram_kernel, out_shape=jax.ShapeDtypeStruct((2, 16, B...  2.64 us
  transfers between devices with their start and end apart: 8, of which 3 were waited for; matrix products, arithmetic and copies ran while one was open for 6% of the time, Pallas kernels for 6%

profile of v3, /device:TPU:1, one launch (start us, length us, event | category | flops | bytes accessed | tf_op | source)
XLA Modules:
  0.0 125.9 jit_solution(16001722055158800913)
XLA Ops:
  0.6 0.0 copy-start.4
  0.6 2.2 %fusion.2 = (bf16[3,192,512]{2,1,0:T(8,128)(2,1)S(1)}, bf16[3,192,512]{2,1,0:T(8,128)(2,1)}) fusion(s32[]{:T(128)S(6)} %select_n.19, bf16[2,192,1024]{2,1,0:T(8,128)(2,1)} %bitcast.13, bf16[1,192,1024]{2,1,0:T(8,128)(2,1)} %bitcast.14, s32[]{:T(128)S(6)} %select_n.18), kind=kLoop, calls=%fused_computation.9 | loop fusion | flops 2359296 | bytes 2359304 | tf_op jit(solution)/shard_map/concatenate | solution.py:221
  2.8 0.0 copy-start.1
  2.8 2.5 %collective-permute-start.1 = (bf16[3,192,512]{2,1,0:T(8,128)(2,1)}, bf16[3,192,512]{2,1,0:T(8,128)(2,1)S(1)}, u32[]{:S(2)}, u32[]{:S(2)}) collective-permute-start(bf16[3,192,512]{2,1,0:T(8,128)(2,1)} %get-tuple-element.8), channel_id=1, source_target_pairs={{0,2},{2,0},{1,3},{3,1},{4,6},{6,4},{5,7},{7,5},{8,10},{10,8},{9,1... | collective-permute-start | bytes 1769480 | tf_op jit(solution)/shard_map/ppermute | solution.py:209
  5.3 0.0 copy-done.4
  5.3 1.3 %broadcast_in_dim.10 = f32[64,6,768]{2,1,0:T(8,128)} broadcast(f32[6,768]{1,0:T(8,128)S(1)} %copy-done.4), dimensions={1,2} | broadcast | bytes 1198080 | tf_op jit(solution)/shard_map/broadcast_in_dim | solution.py:248
  6.6 10.7 %all-to-all-start = ((f32[64,6,768]{2,1,0:T(8,128)}), f32[64,6,768]{2,1,0:T(8,128)S(1)}, u32[]{:S(2)}, u32[]{:S(2)}) async-start(f32[64,6,768]{2,1,0:T(8,128)} %broadcast_in_dim.10), calls=%async_computation | async-start | bytes 3145728 | tf_op jit(solution)/shard_map/all_to_all | solution.py:213
  17.2 0.0 copy-done.1
  17.3 1.3 %collective-permute-start = (bf16[3,192,512]{2,1,0:T(8,128)(2,1)S(1)}, bf16[3,192,512]{2,1,0:T(8,128)(2,1)S(1)}, u32[]{:S(2)}, u32[]{:S(2)}) collective-permute-start(bf16[3,192,512]{2,1,0:T(8,128)(2,1)S(1)} %get-tuple-element.7.own_ref), channel_id=1, source_target_pairs={{0,1},{1,0},{2,3},{3,2},{4,5},{5,4},{6,7},{7,6},{8,9},{9,8},{10,11... | collective-permute-start | bytes 1769480 | tf_op jit(solution)/shard_map/ppermute | solution.py:209
  18.6 0.0 collective-permute-done.1.other_ref
  18.6 0.0 copy-start.2
  18.6 1.4 %collective-permute-start.2 = (bf16[3,192,512]{2,1,0:T(8,128)(2,1)S(1)}, bf16[3,192,512]{2,1,0:T(8,128)(2,1)}, u32[]{:S(2)}, u32[]{:S(2)}) collective-permute-start(bf16[3,192,512]{2,1,0:T(8,128)(2,1)S(1)} %collective-permute-done.1.other_ref), channel_id=1, source_target_pairs={{0,1},{1,0},{2,3},{3,2},{4,5},{5,4},{6,7},{7,6},{8,9},{9,8},{10,11... | collective-permute-start | bytes 1769480 | tf_op jit(solution)/shard_map/ppermute | solution.py:209
  20.0 2.6 %histogram.1.hist_ref = f32[2,16,128]{2,1,0:T(8,128)} custom-call(s32[1]{0:T(128)} %bitcast.3.info, s32[2,8192]{1,0:T(2,128)} %ids_ref.1), custom_call_target="tpu_custom_call" | custom-call | tf_op jit(solution)/shard_map/histogram/pallas_call | solution.py:229
  22.6 0.6 pad_add_fusion.1.info
  23.2 0.0 collective-permute-done.own_c_ref
  23.2 0.0 copy-start.3
  23.2 0.0 collective-permute-done.2.other_c_ref
  23.2 0.0 copy-done.2
  23.2 0.8 copy-done.3
  24.0 4.8 %gram.1 = bf16[64,64,128]{2,1,0:T(8,128)(2,1)} custom-call(s32[2]{0:T(128)} %pad_add_fusion.1.info, f32[2,16,128]{2,1,0:T(8,128)} %histogram.1.hist_ref, bf16[3,192,512]{2,1,0:T(8,128)(2,1)} %copy-done.1, bf16[3,192,512]{2,1,0:T(8,128)(2,1)} %copy-done.3, bf16[3,192,512]{2,1,0:T(8,128)(2,1)} %copy-done.2, ...), custom_call_target="tpu_custom_call" | custom-call | tf_op jit(solution)/shard_map/gram/pallas_call | solution.py:238
  28.8 11.6 %all-to-all-done = f32[64,6,768]{2,1,0:T(8,128)S(1)} async-done(((f32[64,6,768]{2,1,0:T(8,128)}), f32[64,6,768]{2,1,0:T(8,128)S(1)}, u32[]{:S(2)}, u32[]{:S(2)}) %all-to-all-start) | async-done | bytes 1179680 | tf_op jit(solution)/shard_map/all_to_all | solution.py:213
  40.4 15.5 %all-to-all-start.1 = ((bf16[64,64,128]{2,1,0:T(8,128)(2,1)}), bf16[64,64,128]{2,1,0:T(8,128)(2,1)S(1)}, u32[]{:S(2)}, u32[]{:S(2)}) async-start(bf16[64,64,128]{2,1,0:T(8,128)(2,1)} %gram.1), calls=%async_computation.1 | async-start | bytes 2097152 | tf_op jit(solution)/shard_map/all_to_all | solution.py:213
  56.0 18.4 %all-to-all-done.1.in_ref = bf16[64,64,128]{2,1,0:T(8,128)(2,1)S(1)} async-done(((bf16[64,64,128]{2,1,0:T(8,128)(2,1)}), bf16[64,64,128]{2,1,0:T(8,128)(2,1)S(1)}, u32[]{:S(2)}, u32[]{:S(2)}) %all-to-all-start.1) | async-done | bytes 1048608 | tf_op jit(solution)/shard_map/all_to_all | solution.py:213
  74.4 0.0 copy-start
  74.4 1.0 copy-done
  75.3 2.5 %total.1 = bf16[64,64,128]{2,1,0:T(8,128)(2,1)} custom-call(s32[1]{0:T(128)} %bitcast.2.info, bf16[64,64,128]{2,1,0:T(8,128)(2,1)} %copy-done), custom_call_target="tpu_custom_call" | custom-call | tf_op jit(solution)/shard_map/total/pallas_call | solution.py:255
  77.9 5.5 %all-to-all-start.2 = ((bf16[64,64,128]{2,1,0:T(8,128)(2,1)}), bf16[64,64,128]{2,1,0:T(8,128)(2,1)}, u32[]{:S(2)}, u32[]{:S(2)}) async-start(bf16[64,64,128]{2,1,0:T(8,128)(2,1)} %total.1), calls=%async_computation.2 | async-start | bytes 2097152 | tf_op jit(solution)/shard_map/all_to_all | solution.py:213
  83.4 0.0 copy-start.5
  83.4 1.4 %copy.15 = f32[64,6,768]{2,0,1:T(8,128)} copy(f32[64,6,768]{2,1,0:T(8,128)S(1)} %all-to-all-done) | data formatting | bytes 2359296 | tf_op jit(solution)/shard_map/optimization_barrier | solution.py:249
  84.8 1.4 %collective-permute-start.4 = (f32[64,6,768]{2,0,1:T(8,128)}, f32[64,6,768]{2,0,1:T(8,128)S(1)}, u32[]{:S(2)}, u32[]{:S(2)}) collective-permute-start(f32[64,6,768]{2,0,1:T(8,128)} %copy.15), channel_id=1, source_target_pairs={{0,1},{1,0},{2,3},{3,2},{4,5},{5,4},{6,7},{7,6},{8,9},{9,8},{10,11... | collective-permute-start | bytes 3538952 | tf_op jit(solution)/shard_map/ppermute | solution.py:209
  86.1 14.6 %all-to-all-done.2.own_ref = bf16[64,64,128]{2,1,0:T(8,128)(2,1)} async-done(((bf16[64,64,128]{2,1,0:T(8,128)(2,1)}), bf16[64,64,128]{2,1,0:T(8,128)(2,1)}, u32[]{:S(2)}, u32[]{:S(2)}) %all-to-all-start.2) | async-done | bytes 1048608 | tf_op jit(solution)/shard_map/all_to_all | solution.py:213
  100.8 2.2 %collective-permute-start.3 = (bf16[64,64,128]{2,1,0:T(8,128)(2,1)}, bf16[64,64,128]{2,1,0:T(8,128)(2,1)}, u32[]{:S(2)}, u32[]{:S(2)}) collective-permute-start(bf16[64,64,128]{2,1,0:T(8,128)(2,1)} %all-to-all-done.2.own_ref), channel_id=1, source_target_pairs={{0,1},{1,0},{2,3},{3,2},{4,5},{5,4},{6,7},{7,6},{8,9},{9,8},{10,11... | collective-permute-start | bytes 3145736 | tf_op jit(solution)/shard_map/ppermute | solution.py:209
  103.0 0.0 copy-done.5
  103.0 0.8 reshape.17.count_ref
  103.8 0.6 pad_add_fusion.info
  104.4 0.0 collective-permute-done.4
  104.4 0.8 fusion
  105.2 0.3 pad_maximum_fusion
  105.5 0.4 copy.18
  106.0 1.6 %reshape.15.p_ref = f32[768,768]{1,0:T(8,128)} reshape(f32[64,2,6,768]{3,2,1,0:T(8,128)S(1)} %copy.18) | data formatting | bytes 4718592 | tf_op jit(solution)/shard_map/reshape | solution.py:253
  107.6 0.0 collective-permute-done.3.other_ref
  107.6 18.3 %finish.1 = (f32[6,768]{1,0:T(8,128)}, f32[384,768]{1,0:T(8,128)}) custom-call(s32[2]{0:T(128)} %pad_add_fusion.info, bf16[64,64,128]{2,1,0:T(8,128)(2,1)} %all-to-all-done.2.own_ref, bf16[64,64,128]{2,1,0:T(8,128)(2,1)} %collective-permute-done.3.other_ref, f32[768,768]{1,0:T(8,128)} %reshape.15.p_ref, f32[6,768]{1,0:T(8,128)} %p_mom_ref.1, ...), custom_call_target="tpu_custom_call" | custom-call | tf_op jit(solution)/shard_map/finish/pallas_call | solution.py:266
Async XLA Ops:
  0.6 4.7 %copy-start.4 = (f32[6,768]{1,0:T(8,128)S(1)}, f32[6,768]{1,0:T(8,128)}, u32[]{:S(2)}) copy-start(f32[6,768]{1,0:T(8,128)} %param.11) | copy-start | bytes 55300
  2.8 14.4 %copy-start.1 = (bf16[3,192,512]{2,1,0:T(8,128)(2,1)}, bf16[3,192,512]{2,1,0:T(8,128)(2,1)S(1)}, u32[]{:S(2)}) copy-start(bf16[3,192,512]{2,1,0:T(8,128)(2,1)S(1)} %get-tuple-element.7.own_ref) | copy-start | bytes 1769476
  2.8 15.8 %collective-permute-start.1 = (bf16[3,192,512]{2,1,0:T(8,128)(2,1)}, bf16[3,192,512]{2,1,0:T(8,128)(2,1)S(1)}, u32[]{:S(2)}, u32[]{:S(2)}) collective-permute-start(bf16[3,192,512]{2,1,0:T(8,128)(2,1)} %get-tuple-element.8), channel_id=1, source_target_pairs={{0,2},{2,0},{1,3},{3,1},{4,6},{6,4},{5,7},{7,5},{8,10},{10,8},{9,1... | collective-permute-start | bytes 1769480 | tf_op jit(solution)/shard_map/ppermute | solution.py:209
  6.6 33.9 %all-to-all-start = ((f32[64,6,768]{2,1,0:T(8,128)}), f32[64,6,768]{2,1,0:T(8,128)S(1)}, u32[]{:S(2)}, u32[]{:S(2)}) async-start(f32[64,6,768]{2,1,0:T(8,128)} %broadcast_in_dim.10), calls=%async_computation | async-start | bytes 3145728 | tf_op jit(solution)/shard_map/all_to_all | solution.py:213
  17.3 5.9 %collective-permute-start = (bf16[3,192,512]{2,1,0:T(8,128)(2,1)S(1)}, bf16[3,192,512]{2,1,0:T(8,128)(2,1)S(1)}, u32[]{:S(2)}, u32[]{:S(2)}) collective-permute-start(bf16[3,192,512]{2,1,0:T(8,128)(2,1)S(1)} %get-tuple-element.7.own_ref), channel_id=1, source_target_pairs={{0,1},{1,0},{2,3},{3,2},{4,5},{5,4},{6,7},{7,6},{8,9},{9,8},{10,11... | collective-permute-start | bytes 1769480 | tf_op jit(solution)/shard_map/ppermute | solution.py:209
  18.6 4.6 %copy-start.2 = (bf16[3,192,512]{2,1,0:T(8,128)(2,1)}, bf16[3,192,512]{2,1,0:T(8,128)(2,1)S(1)}, u32[]{:S(2)}) copy-start(bf16[3,192,512]{2,1,0:T(8,128)(2,1)S(1)} %collective-permute-done.1.other_ref) | copy-start | bytes 1769476
  18.6 4.6 %collective-permute-start.2 = (bf16[3,192,512]{2,1,0:T(8,128)(2,1)S(1)}, bf16[3,192,512]{2,1,0:T(8,128)(2,1)}, u32[]{:S(2)}, u32[]{:S(2)}) collective-permute-start(bf16[3,192,512]{2,1,0:T(8,128)(2,1)S(1)} %collective-permute-done.1.other_ref), channel_id=1, source_target_pairs={{0,1},{1,0},{2,3},{3,2},{4,5},{5,4},{6,7},{7,6},{8,9},{9,8},{10,11... | collective-permute-start | bytes 1769480 | tf_op jit(solution)/shard_map/ppermute | solution.py:209
  23.2 0.8 copy-start.3
  40.4 33.9 %all-to-all-start.1 = ((bf16[64,64,128]{2,1,0:T(8,128)(2,1)}), bf16[64,64,128]{2,1,0:T(8,128)(2,1)S(1)}, u32[]{:S(2)}, u32[]{:S(2)}) async-start(bf16[64,64,128]{2,1,0:T(8,128)(2,1)} %gram.1), calls=%async_computation.1 | async-start | bytes 2097152 | tf_op jit(solution)/shard_map/all_to_all | solution.py:213
  74.4 1.0 copy-start
  77.9 22.9 %all-to-all-start.2 = ((bf16[64,64,128]{2,1,0:T(8,128)(2,1)}), bf16[64,64,128]{2,1,0:T(8,128)(2,1)}, u32[]{:S(2)}, u32[]{:S(2)}) async-start(bf16[64,64,128]{2,1,0:T(8,128)(2,1)} %total.1), calls=%async_computation.2 | async-start | bytes 2097152 | tf_op jit(solution)/shard_map/all_to_all | solution.py:213
  83.4 19.6 %copy-start.5 = (s32[384]{0:T(512)S(1)}, s32[384]{0:T(512)}, u32[]{:S(2)}) copy-start(s32[384]{0:T(512)} %param.15) | copy-start | bytes 4612
  84.8 19.6 %collective-permute-start.4 = (f32[64,6,768]{2,0,1:T(8,128)}, f32[64,6,768]{2,0,1:T(8,128)S(1)}, u32[]{:S(2)}, u32[]{:S(2)}) collective-permute-start(f32[64,6,768]{2,0,1:T(8,128)} %copy.15), channel_id=1, source_target_pairs={{0,1},{1,0},{2,3},{3,2},{4,5},{5,4},{6,7},{7,6},{8,9},{9,8},{10,11... | collective-permute-start | bytes 3538952 | tf_op jit(solution)/shard_map/ppermute | solution.py:209
  100.8 6.8 %collective-permute-start.3 = (bf16[64,64,128]{2,1,0:T(8,128)(2,1)}, bf16[64,64,128]{2,1,0:T(8,128)(2,1)}, u32[]{:S(2)}, u32[]{:S(2)}) collective-permute-start(bf16[64,64,128]{2,1,0:T(8,128)(2,1)} %all-to-all-done.2.own_ref), channel_id=1, source_target_pairs={{0,1},{1,0},{2,3},{3,2},{4,5},{5,4},{6,7},{7,6},{8,9},{9,8},{10,11... | collective-permute-start | bytes 3145736 | tf_op jit(solution)/shard_map/ppermute | solution.py:209

commit v4 on v3

--- a/solution.py
+++ b/solution.py
@@ -246,7 +246,6 @@
     )(jnp.stack([zl, core]), hist, keep, keep_c, other, other_c, token_counts.reshape(3, BLK))
 
     p_own = exchange(jnp.broadcast_to(p_rows[None], (CHIPS,) + proj_grad.shape))
-    parts, p_own = lax.optimization_barrier((parts, p_own))
     arrived = exchange(parts)
     p_other = to_other(p_own, "c")
     p_pair = jnp.stack([jnp.where(core == 0, p_own, p_other), jnp.where(core == 0, p_other, p_own)], axis=1)

time: 126 us -> 135 us (1.071)
  blocking collectives: 0 us -> 29.6 us
  starting transfers between devices: 40.4 us -> 21.3 us
    all_to_all x0 -> x1, blocking collectives: none -> 29.6 us  [exchange(): return lax.all_to_all(x, CHIP_AXES, split_axis=0, concat_axis=0, tiled=True)]
    all_to_all x3 -> x2, starting transfers between devices: 31.7 us -> 10.2 us  [exchange(): return lax.all_to_all(x, CHIP_AXES, split_axis=0, concat_axis=0, tiled=True)]
    all_to_all x3 -> x2, waiting for transfers between devices: 44.7 us -> 32.3 us  [exchange(): return lax.all_to_all(x, CHIP_AXES, split_axis=0, concat_axis=0, tiled=True)]
    ppermute x5, waiting for transfers between devices: 0.01 us -> 12.1 us  [to_other(): return lax.ppermute(x, axis, [(0, 1), (1, 0)])]
    ppermute x5, starting transfers between devices: 8.76 us -> 11.1 us  [to_other(): return lax.ppermute(x, axis, [(0, 1), (1, 0)])]
    all_to_all x0 -> x1, local copies, waits for them, and re-layouts: none -> 1.38 us  [exchange(): return lax.all_to_all(x, CHIP_AXES, split_axis=0, concat_axis=0, tiled=True)]
    optimization_barrier x1 -> x0, local copies, waits for them, and re-layouts: 1.38 us -> none  [per_device(): parts, p_own = lax.optimization_barrier((parts, p_own))]
  transfers between devices with their start and end apart: 8 -> 7, of which waited for: 3 -> 3; matrix products, arithmetic and copies ran while one was open for 6% -> 5% of each run, Pallas kernels for 6% -> 4%
where the time goes in v4:
time: 135 us
  waiting for transfers between devices  44.4 us (33%)
  blocking collectives  29.6 us (22%)
  Pallas kernels  28.3 us (21%)
  starting transfers between devices  21.3 us (16%)
  local copies, waits for them, and re-layouts  6.54 us (5%)
  other arithmetic  3.68 us (3%)
    all_to_all x2, waiting for transfers between devices, exchange(): return lax.all_to_all(x, CHIP_AXES, split_axis=0, concat_axis=0, tiled=True)  32.3 us
    all_to_all x1, blocking collectives, exchange(): return lax.all_to_all(x, CHIP_AXES, split_axis=0, concat_axis=0, tiled=True)  29.6 us
    pallas_call x1, Pallas kernels, per_device(): pl.pallas_call(finish_kernel, out_shape=(jax.ShapeDtypeStruct(proj_moment...  18.3 us
    ppermute x5, waiting for transfers between devices, to_other(): return lax.ppermute(x, axis, [(0, 1), (1, 0)])  12.1 us
    ppermute x5, starting transfers between devices, to_other(): return lax.ppermute(x, axis, [(0, 1), (1, 0)])  11.1 us
    all_to_all x2, starting transfers between devices, exchange(): return lax.all_to_all(x, CHIP_AXES, split_axis=0, concat_axis=0, tiled=True)  10.2 us
    pallas_call x1, Pallas kernels, per_device(): pl.pallas_call(gram_kernel, out_shape=jax.ShapeDtypeStruct((CHIPS, HALF,...  4.83 us
  transfers between devices with their start and end apart: 7, of which 3 were waited for; matrix products, arithmetic and copies ran while one was open for 5% of the time, Pallas kernels for 4%

profile of v4, /device:TPU:1, one launch (start us, length us, event | category | flops | bytes accessed | tf_op | source)
XLA Modules:
  0.0 134.6 jit_solution(8463413340193847083)
XLA Ops:
  0.6 1.3 fusion.2
  1.9 0.0 copy-start
  2.0 2.5 %collective-permute-start.1 = (bf16[3,192,512]{2,1,0:T(8,128)(2,1)S(1)}, bf16[3,192,512]{2,1,0:T(8,128)(2,1)S(1)}, u32[]{:S(2)}, u32[]{:S(2)}) collective-permute-start(bf16[3,192,512]{2,1,0:T(8,128)(2,1)S(1)} %get-tuple-element.6), channel_id=1, source_target_pairs={{0,2},{2,0},{1,3},{3,1},{4,6},{6,4},{5,7},{7,5},{8,10},{10,8},{9,1... | collective-permute-start | bytes 1769480 | tf_op jit(solution)/shard_map/ppermute | solution.py:209
  4.5 1.0 collective-permute-start
  5.5 12.1 %collective-permute-done.1.other_ref = bf16[3,192,512]{2,1,0:T(8,128)(2,1)S(1)} collective-permute-done((bf16[3,192,512]{2,1,0:T(8,128)(2,1)S(1)}, bf16[3,192,512]{2,1,0:T(8,128)(2,1)S(1)}, u32[]{:S(2)}, u32[]{:S(2)}) %collective-permute-start.1) | collective-permute-done | bytes 589856 | tf_op jit(solution)/shard_map/ppermute | solution.py:209
  17.5 0.0 copy-start.1
  17.5 1.3 collective-permute-start.2
  18.8 2.6 %histogram.1.hist_ref = f32[2,16,128]{2,1,0:T(8,128)} custom-call(s32[1]{0:T(128)} %bitcast.3.info, s32[2,8192]{1,0:T(2,128)} %ids_ref.1), custom_call_target="tpu_custom_call" | custom-call | tf_op jit(solution)/shard_map/histogram/pallas_call | solution.py:229
  21.4 0.7 pad_add_fusion.1.info
  22.1 0.0 collective-permute-done.own_c_ref
  22.1 0.0 copy-start.2
  22.1 0.0 collective-permute-done.2.other_c_ref
  22.1 0.0 copy-start.3
  22.1 0.0 copy-done
  22.1 0.0 copy-done.1
  22.1 0.8 copy-done.2
  22.9 0.2 copy-done.3
  23.1 4.8 %gram.1 = bf16[64,64,128]{2,1,0:T(8,128)(2,1)} custom-call(s32[2]{0:T(128)} %pad_add_fusion.1.info, f32[2,16,128]{2,1,0:T(8,128)} %histogram.1.hist_ref, bf16[3,192,512]{2,1,0:T(8,128)(2,1)} %copy-done, bf16[3,192,512]{2,1,0:T(8,128)(2,1)} %copy-done.2, bf16[3,192,512]{2,1,0:T(8,128)(2,1)} %copy-done.1, bf16[3,192,512]{2,1,0:T(8,128)(2,1)} %copy-done.3, ...), custom_call_target="tpu_custom_call" | custom-call | tf_op jit(solution)/shard_map/gram/pallas_call | solution.py:238
  27.9 0.0 copy-start.4
  27.9 29.6 %all_to_all.15.in_ref = bf16[64,64,128]{2,1,0:T(8,128)(2,1)} all-to-all(bf16[64,64,128]{2,1,0:T(8,128)(2,1)} %gram.1), channel_id=1, replica_groups=mesh['y'=4,'zh'=2,'x'=4,'zl'=2,'c'=2] {'y','zh','x','zl'}, dimensions={0} | all-to-all | bytes 2097152 | tf_op jit(solution)/shard_map/all_to_all | solution.py:213
  57.6 0.0 copy-done.4
  57.6 1.3 broadcast_in_dim.10
  58.9 4.7 %all-to-all-start.2 = ((f32[64,6,768]{2,1,0:T(8,128)}), f32[64,6,768]{2,1,0:T(8,128)S(1)}, u32[]{:S(2)}, u32[]{:S(2)}) async-start(f32[64,6,768]{2,1,0:T(8,128)} %broadcast_in_dim.10), calls=%async_computation.2 | async-start | bytes 3145728 | tf_op jit(solution)/shard_map/all_to_all | solution.py:213
  63.5 2.5 %total.1 = bf16[64,64,128]{2,1,0:T(8,128)(2,1)} custom-call(s32[1]{0:T(128)} %bitcast.2.info, bf16[64,64,128]{2,1,0:T(8,128)(2,1)} %all_to_all.15.in_ref), custom_call_target="tpu_custom_call" | custom-call | tf_op jit(solution)/shard_map/total/pallas_call | solution.py:254
  66.1 20.4 %all-to-all-done.2 = f32[64,6,768]{2,1,0:T(8,128)S(1)} async-done(((f32[64,6,768]{2,1,0:T(8,128)}), f32[64,6,768]{2,1,0:T(8,128)S(1)}, u32[]{:S(2)}, u32[]{:S(2)}) %all-to-all-start.2) | async-done | bytes 1179680 | tf_op jit(solution)/shard_map/all_to_all | solution.py:213
  86.5 5.5 %all-to-all-start.1 = ((bf16[64,64,128]{2,1,0:T(8,128)(2,1)}), bf16[64,64,128]{2,1,0:T(8,128)(2,1)}, u32[]{:S(2)}, u32[]{:S(2)}) async-start(bf16[64,64,128]{2,1,0:T(8,128)(2,1)} %total.1), calls=%async_computation.1 | async-start | bytes 2097152 | tf_op jit(solution)/shard_map/all_to_all | solution.py:213
  92.0 0.0 copy-start.5
  92.0 1.4 %copy.15 = f32[64,6,768]{2,0,1:T(8,128)} copy(f32[64,6,768]{2,1,0:T(8,128)S(1)} %all-to-all-done.2) | data formatting | bytes 2359296 | tf_op jit(solution)/shard_map/all_to_all | solution.py:213
  93.4 2.5 %collective-permute-start.4 = (f32[64,6,768]{2,0,1:T(8,128)}, f32[64,6,768]{2,0,1:T(8,128)S(1)}, u32[]{:S(2)}, u32[]{:S(2)}) collective-permute-start(f32[64,6,768]{2,0,1:T(8,128)} %copy.15), channel_id=1, source_target_pairs={{0,1},{1,0},{2,3},{3,2},{4,5},{5,4},{6,7},{7,6},{8,9},{9,8},{10,11... | collective-permute-start | bytes 3538952 | tf_op jit(solution)/shard_map/ppermute | solution.py:209
  95.9 11.9 %all-to-all-done.1.own_ref = bf16[64,64,128]{2,1,0:T(8,128)(2,1)} async-done(((bf16[64,64,128]{2,1,0:T(8,128)(2,1)}), bf16[64,64,128]{2,1,0:T(8,128)(2,1)}, u32[]{:S(2)}, u32[]{:S(2)}) %all-to-all-start.1) | async-done | bytes 1048608 | tf_op jit(solution)/shard_map/all_to_all | solution.py:213
  107.8 3.9 %collective-permute-start.3 = (bf16[64,64,128]{2,1,0:T(8,128)(2,1)}, bf16[64,64,128]{2,1,0:T(8,128)(2,1)}, u32[]{:S(2)}, u32[]{:S(2)}) collective-permute-start(bf16[64,64,128]{2,1,0:T(8,128)(2,1)} %all-to-all-done.1.own_ref), channel_id=1, source_target_pairs={{0,1},{1,0},{2,3},{3,2},{4,5},{5,4},{6,7},{7,6},{8,9},{9,8},{10,11... | collective-permute-start | bytes 3145736 | tf_op jit(solution)/shard_map/ppermute | solution.py:209
  111.6 0.0 copy-done.5
  111.6 0.8 reshape.17.count_ref
  112.4 0.6 pad_add_fusion.info
  113.0 0.0 collective-permute-done.4
  113.0 0.8 fusion
  113.9 0.3 pad_maximum_fusion
  114.2 0.4 copy.18
  114.6 1.6 %reshape.15.p_ref = f32[768,768]{1,0:T(8,128)} reshape(f32[64,2,6,768]{3,2,1,0:T(8,128)S(1)} %copy.18) | data formatting | bytes 4718592 | tf_op jit(solution)/shard_map/reshape | solution.py:252
  116.3 0.0 collective-permute-done.3.other_ref
  116.3 18.3 %finish.1 = (f32[6,768]{1,0:T(8,128)}, f32[384,768]{1,0:T(8,128)}) custom-call(s32[2]{0:T(128)} %pad_add_fusion.info, bf16[64,64,128]{2,1,0:T(8,128)(2,1)} %all-to-all-done.1.own_ref, bf16[64,64,128]{2,1,0:T(8,128)(2,1)} %collective-permute-done.3.other_ref, f32[768,768]{1,0:T(8,128)} %reshape.15.p_ref, f32[6,768]{1,0:T(8,128)} %p_mom_ref.1, ...), custom_call_target="tpu_custom_call" | custom-call | tf_op jit(solution)/shard_map/finish/pallas_call | solution.py:265
Async XLA Ops:
  1.9 20.2 %copy-start = (bf16[3,192,512]{2,1,0:T(8,128)(2,1)}, bf16[3,192,512]{2,1,0:T(8,128)(2,1)S(1)}, u32[]{:S(2)}) copy-start(bf16[3,192,512]{2,1,0:T(8,128)(2,1)S(1)} %get-tuple-element.5.own_ref) | copy-start | bytes 1769476
  2.0 15.6 %collective-permute-start.1 = (bf16[3,192,512]{2,1,0:T(8,128)(2,1)S(1)}, bf16[3,192,512]{2,1,0:T(8,128)(2,1)S(1)}, u32[]{:S(2)}, u32[]{:S(2)}) collective-permute-start(bf16[3,192,512]{2,1,0:T(8,128)(2,1)S(1)} %get-tuple-element.6), channel_id=1, source_target_pairs={{0,2},{2,0},{1,3},{3,1},{4,6},{6,4},{5,7},{7,5},{8,10},{10,8},{9,1... | collective-permute-start | bytes 1769480 | tf_op jit(solution)/shard_map/ppermute | solution.py:209
  4.5 17.6 %collective-permute-start = (bf16[3,192,512]{2,1,0:T(8,128)(2,1)S(1)}, bf16[3,192,512]{2,1,0:T(8,128)(2,1)S(1)}, u32[]{:S(2)}, u32[]{:S(2)}) collective-permute-start(bf16[3,192,512]{2,1,0:T(8,128)(2,1)S(1)} %get-tuple-element.5.own_ref), channel_id=1, source_target_pairs={{0,1},{1,0},{2,3},{3,2},{4,5},{5,4},{6,7},{7,6},{8,9},{9,8},{10,11... | collective-permute-start | bytes 1769480 | tf_op jit(solution)/shard_map/ppermute | solution.py:209
  17.5 4.6 %copy-start.1 = (bf16[3,192,512]{2,1,0:T(8,128)(2,1)}, bf16[3,192,512]{2,1,0:T(8,128)(2,1)S(1)}, u32[]{:S(2)}) copy-start(bf16[3,192,512]{2,1,0:T(8,128)(2,1)S(1)} %collective-permute-done.1.other_ref) | copy-start | bytes 1769476
  17.5 4.6 %collective-permute-start.2 = (bf16[3,192,512]{2,1,0:T(8,128)(2,1)S(1)}, bf16[3,192,512]{2,1,0:T(8,128)(2,1)S(1)}, u32[]{:S(2)}, u32[]{:S(2)}) collective-permute-start(bf16[3,192,512]{2,1,0:T(8,128)(2,1)S(1)} %collective-permute-done.1.other_ref), channel_id=1, source_target_pairs={{0,1},{1,0},{2,3},{3,2},{4,5},{5,4},{6,7},{7,6},{8,9},{9,8},{10,11... | collective-permute-start | bytes 1769480 | tf_op jit(solution)/shard_map/ppermute | solution.py:209
  22.1 0.8 copy-start.2
  22.1 1.0 copy-start.3
  27.9 29.6 %copy-start.4 = (f32[6,768]{1,0:T(8,128)S(1)}, f32[6,768]{1,0:T(8,128)}, u32[]{:S(2)}) copy-start(f32[6,768]{1,0:T(8,128)} %param.11) | copy-start | bytes 55300
  58.9 27.6 %all-to-all-start.2 = ((f32[64,6,768]{2,1,0:T(8,128)}), f32[64,6,768]{2,1,0:T(8,128)S(1)}, u32[]{:S(2)}, u32[]{:S(2)}) async-start(f32[64,6,768]{2,1,0:T(8,128)} %broadcast_in_dim.10), calls=%async_computation.2 | async-start | bytes 3145728 | tf_op jit(solution)/shard_map/all_to_all | solution.py:213
  86.5 21.3 %all-to-all-start.1 = ((bf16[64,64,128]{2,1,0:T(8,128)(2,1)}), bf16[64,64,128]{2,1,0:T(8,128)(2,1)}, u32[]{:S(2)}, u32[]{:S(2)}) async-start(bf16[64,64,128]{2,1,0:T(8,128)(2,1)} %total.1), calls=%async_computation.1 | async-start | bytes 2097152 | tf_op jit(solution)/shard_map/all_to_all | solution.py:213
  92.0 19.6 %copy-start.5 = (s32[384]{0:T(512)S(1)}, s32[384]{0:T(512)}, u32[]{:S(2)}) copy-start(s32[384]{0:T(512)} %param.15) | copy-start | bytes 4612
  93.4 19.6 %collective-permute-start.4 = (f32[64,6,768]{2,0,1:T(8,128)}, f32[64,6,768]{2,0,1:T(8,128)S(1)}, u32[]{:S(2)}, u32[]{:S(2)}) collective-permute-start(f32[64,6,768]{2,0,1:T(8,128)} %copy.15), channel_id=1, source_target_pairs={{0,1},{1,0},{2,3},{3,2},{4,5},{5,4},{6,7},{7,6},{8,9},{9,8},{10,11... | collective-permute-start | bytes 3538952 | tf_op jit(solution)/shard_map/ppermute | solution.py:209
  107.8 8.5 %collective-permute-start.3 = (bf16[64,64,128]{2,1,0:T(8,128)(2,1)}, bf16[64,64,128]{2,1,0:T(8,128)(2,1)}, u32[]{:S(2)}, u32[]{:S(2)}) collective-permute-start(bf16[64,64,128]{2,1,0:T(8,128)(2,1)} %all-to-all-done.1.own_ref), channel_id=1, source_target_pairs={{0,1},{1,0},{2,3},{3,2},{4,5},{5,4},{6,7},{7,6},{8,9},{9,8},{10,11... | collective-permute-start | bytes 3145736 | tf_op jit(solution)/shard_map/ppermute | solution.py:209
